TPU v7x, 256 devices: a whole 4x4x8 slice. The times are simulated.
256 devices in a mesh: dp: 16 (over z_lo, x), seq: 16 (over z_hi, y, core).
Axes of the slice: x: 4, y: 4, z: 8 (z_hi: 2, z_lo: 4; z = z_hi * 4 + z_lo), core: 2. Of those that a mesh axis runs over, the one named last changes fastest.
Arguments:
- queries: bfloat16 [16, 2048, 2048], P('dp', 'seq'), may hold values from -5 to 5
- key_states: bfloat16 [16, 2048, 2048], P('dp', 'seq'), may hold values from -5 to 5
- value_states: bfloat16 [16, 2048, 2048], P('dp', 'seq'), may hold values from -6 to 6
- residual: bfloat16 [16, 2048, 2048], P('dp', 'seq'), may hold values from -6 to 6
- enc_hidden: bfloat16 [16, 2048, 1536], P('dp', 'seq'), may hold values from -6 to 6
- enc_gain: float32 [1536], replicated, may hold values from 0.1 to 1.9
- enc_bias: float32 [1536], replicated, may hold values from -0.5 to 0.5
- feature_target: int32 [16, 2048], P('dp', 'seq'), may hold values from 0 to 2047, as said below
- timestep: int32 [16], P('dp'), may hold values from 0 to 999
- gate_weight: bfloat16 [256, 2048], P('dp'), may hold values from -0.375 to 0.375
- lift_weight: bfloat16 [2048, 1024], P('dp'), may hold values from -0.125 to 0.125
- out_weight: bfloat16 [1024, 1536], P('dp'), may hold values from -0.1875 to 0.1875
Outputs:
- d_queries: bfloat16 [16, 2048, 2048], P('dp', 'seq')
- d_keys: bfloat16 [16, 2048, 2048], P('dp', 'seq')
- d_values: bfloat16 [16, 2048, 2048], P('dp', 'seq')
- grad_gate: float32 [256, 2048], P('dp')
- grad_lift: float32 [2048, 1024], P('dp')
- grad_out: float32 [1024, 1536], P('dp')
Inputs may be any that keep to these rules, and one draw needn't show every extreme that they name: For each clip, feature_target is a permutation of its 2048 token positions. The 128 encoder rows of one device of seq target at most 16 tokens held by any one device of seq, and exactly 16 for some.
All inputs are finite; a program needn't handle non-finite values.
Results may differ from a plain program's by a relative error of at most 0.02.
Values may be sent and summed in bfloat16 or wider, within the bound.
A program may use at most 128 MiB of HBM per device.

v0:
```python
import math

import jax
import jax.numpy as jnp
from jax import lax
from jax.sharding import PartitionSpec as P

HD = 128
ZD = 1536
TEMB = 256


EPSILON = 1e-06


def laid_out(blocks, dim):
    blocks = jnp.moveaxis(blocks, 0, dim)
    lengths = blocks.shape
    return blocks.reshape(*lengths[:dim], lengths[dim] * lengths[dim + 1], *lengths[dim + 2 :])


def gather_packed(arrays, axis, dims):
    line = jnp.concatenate([a.reshape(-1) for a in arrays])
    lines, at, done = (lax.all_gather(line, axis), 0, [])
    for a, dim in zip(arrays, dims):
        blocks = lines[:, at : at + a.size].reshape(-1, *a.shape)
        done.append(laid_out(blocks, dim))
        at += a.size
    return tuple(done)


def embed_time(timestep):
    half_width = TEMB // 2
    frequency = jnp.exp(
        -math.log(10000.0) * jnp.arange(half_width).astype(jnp.float32) / half_width
    )
    angles = timestep.astype(jnp.float32)[:, None] * frequency[None, :]
    return jnp.concatenate([jnp.cos(angles), jnp.sin(angles)], axis=1).astype(jnp.bfloat16)


def encoder_norm(hidden, enc_gain, enc_bias):
    widened = hidden.astype(jnp.float32)
    centred = widened - jnp.mean(widened, axis=-1, keepdims=True)
    variance = jnp.mean(centred * centred, axis=-1, keepdims=True)
    return (centred * lax.rsqrt(variance + EPSILON) * enc_gain + enc_bias).astype(jnp.bfloat16)


def soft_scores(query_block, key_heads):
    scores = jnp.einsum(
        "bhd,lhd->hbl", query_block, key_heads, preferred_element_type=jnp.float32
    ) * HD ** (-0.5)
    shifted = jnp.exp(scores - jnp.max(scores, axis=-1, keepdims=True))
    return shifted / jnp.sum(shifted, axis=-1, keepdims=True)


def split_blocks(array):
    length = array.shape[0]
    block_rows = min(length, 512)
    return array.reshape(length // block_rows, block_rows, array.shape[1], array.shape[2])


def attention_forward(query_heads, key_heads, value_heads):

    def one_block(query_block):
        chances = soft_scores(query_block, key_heads).astype(jnp.bfloat16)
        return jnp.einsum(
            "hbl,lhd->bhd", chances, value_heads, preferred_element_type=jnp.float32
        ).astype(jnp.bfloat16)

    mixed = lax.map(one_block, split_blocks(query_heads))
    return mixed.reshape(query_heads.shape[0], -1)


def attention_backward(query_heads, key_heads, value_heads, grad_heads):

    def one_block(carried, pieces):
        grad_keys, grad_values = carried
        query_block, grad_block = pieces
        chances = soft_scores(query_block, key_heads)
        grad_chances = jnp.einsum(
            "bhd,lhd->hbl", grad_block, value_heads, preferred_element_type=jnp.float32
        )
        grad_values = grad_values + jnp.einsum(
            "hbl,bhd->lhd",
            chances.astype(jnp.bfloat16),
            grad_block,
            preferred_element_type=jnp.float32,
        )
        inner_sum = jnp.sum(grad_chances * chances, axis=-1, keepdims=True)
        grad_scores = (chances * (grad_chances - inner_sum) * HD ** (-0.5)).astype(jnp.bfloat16)
        grad_query = jnp.einsum(
            "hbl,lhd->bhd", grad_scores, key_heads, preferred_element_type=jnp.float32
        )
        grad_keys = grad_keys + jnp.einsum(
            "hbl,bhd->lhd", grad_scores, query_block, preferred_element_type=jnp.float32
        )
        return ((grad_keys, grad_values), grad_query.astype(jnp.bfloat16))

    zeros = jnp.zeros(key_heads.shape, jnp.float32)
    carried, grad_queries = lax.scan(
        one_block, (zeros, zeros), (split_blocks(query_heads), split_blocks(grad_heads))
    )
    length = query_heads.shape[0]
    return (
        grad_queries.reshape(length, -1),
        carried[0].reshape(length, -1).astype(jnp.bfloat16),
        carried[1].reshape(length, -1).astype(jnp.bfloat16),
    )


def shards(
    queries,
    key_states,
    value_states,
    residual,
    enc_hidden,
    enc_gain,
    enc_bias,
    feature_target,
    timestep,
    gate_weight,
    lift_weight,
    out_weight,
):
    groups = lax.axis_size("seq")
    tokens_here = queries.shape[1]
    z_width = enc_hidden.shape[2]
    capacity = 2 * tokens_here // groups
    normed = encoder_norm(enc_hidden[0], enc_gain, enc_bias)
    targets = feature_target[0]
    owning = targets // tokens_here
    onehot = (owning[:, None] == jnp.arange(groups)[None, :]).astype(jnp.int32)
    ranked = jnp.sum((jnp.cumsum(onehot, axis=0) - onehot) * onehot, axis=1)
    slotted = owning * capacity + ranked
    send_rows = jnp.zeros((groups * capacity, z_width), jnp.bfloat16).at[slotted].set(normed)
    send_places = (
        jnp.zeros((groups * capacity,), jnp.int32).at[slotted].set(targets % tokens_here + 1)
    )
    got_rows, got_places = (
        lax.all_to_all(
            send_rows.reshape(groups, capacity, z_width),
            "seq",
            split_axis=0,
            concat_axis=0,
            tiled=True,
        ),
        lax.all_to_all(
            send_places.reshape(groups, capacity), "seq", split_axis=0, concat_axis=0, tiled=True
        ),
    )
    aligned = (
        jnp.zeros((tokens_here + 1, z_width), jnp.bfloat16)
        .at[got_places.reshape(-1)]
        .set(got_rows.reshape(-1, z_width))[1:]
    )
    gate_full, lift_full, out_full = gather_packed(
        (gate_weight, lift_weight, out_weight), "dp", (0, 0, 0)
    )
    embedded = embed_time(timestep)
    gating = jnp.dot(embedded, gate_full, preferred_element_type=jnp.float32)
    query_heads, key_heads, value_heads = (
        lax.all_to_all(queries[0], "seq", split_axis=1, concat_axis=0, tiled=True),
        lax.all_to_all(key_states[0], "seq", split_axis=1, concat_axis=0, tiled=True),
        lax.all_to_all(value_states[0], "seq", split_axis=1, concat_axis=0, tiled=True),
    )
    local_width = query_heads.shape[1]

    def heads_of(array):
        return array.reshape(array.shape[0], local_width // HD, HD)

    mixed_heads = attention_forward(
        heads_of(query_heads), heads_of(key_heads), heads_of(value_heads)
    )
    mixed = lax.all_to_all(mixed_heads, "seq", split_axis=0, concat_axis=1, tiled=True)
    mixed_wide = mixed.astype(jnp.float32)
    hidden = (residual[0].astype(jnp.float32) + gating * mixed_wide).astype(jnp.bfloat16)
    lifted = jnp.dot(hidden, lift_full, preferred_element_type=jnp.float32)
    sigmoid_lift = jax.nn.sigmoid(lifted)
    activated = (lifted * sigmoid_lift).astype(jnp.bfloat16)
    predicted = jnp.dot(activated, out_full, preferred_element_type=jnp.float32)
    target_wide = aligned.astype(jnp.float32)
    pred_norm = jnp.sqrt(jnp.sum(predicted * predicted, axis=1, keepdims=True) + EPSILON)
    target_norm = jnp.sqrt(jnp.sum(target_wide * target_wide, axis=1, keepdims=True) + EPSILON)
    cosine = jnp.sum(predicted * target_wide, axis=1, keepdims=True) / (pred_norm * target_norm)
    grad_pred = (
        -1.0
        * ZD
        * (target_wide / (pred_norm * target_norm) - cosine * predicted / (pred_norm * pred_norm))
    ).astype(jnp.bfloat16)
    part_out = jnp.einsum("tp,tz->pz", activated, grad_pred, preferred_element_type=jnp.float32)
    grad_act = jnp.einsum("tz,pz->tp", grad_pred, out_full, preferred_element_type=jnp.float32)
    grad_lifted = (grad_act * sigmoid_lift * (1.0 + lifted * (1.0 - sigmoid_lift))).astype(
        jnp.bfloat16
    )
    part_lift = jnp.einsum("tf,tp->fp", hidden, grad_lifted, preferred_element_type=jnp.float32)
    grad_hidden = jnp.einsum(
        "tp,fp->tf", grad_lifted, lift_full, preferred_element_type=jnp.float32
    )
    grad_mixed = (gating * grad_hidden).astype(jnp.bfloat16)
    grad_gating = jnp.sum(grad_hidden * mixed_wide, axis=0, keepdims=True)
    part_gate = jnp.dot(
        embedded.astype(jnp.float32).T, grad_gating, precision=lax.Precision.HIGHEST
    )
    grad_heads = lax.all_to_all(grad_mixed, "seq", split_axis=1, concat_axis=0, tiled=True)
    grad_query, grad_key, grad_value = attention_backward(
        heads_of(query_heads), heads_of(key_heads), heads_of(value_heads), heads_of(grad_heads)
    )
    d_queries, d_keys, d_values = (
        lax.all_to_all(grad_query, "seq", split_axis=0, concat_axis=1, tiled=True),
        lax.all_to_all(grad_key, "seq", split_axis=0, concat_axis=1, tiled=True),
        lax.all_to_all(grad_value, "seq", split_axis=0, concat_axis=1, tiled=True),
    )
    share_gate, share_lift, share_out = (
        lax.psum_scatter(
            part_gate.astype(jnp.bfloat16), "dp", scatter_dimension=0, tiled=True
        ).astype(jnp.float32),
        lax.psum_scatter(
            part_lift.astype(jnp.bfloat16), "dp", scatter_dimension=0, tiled=True
        ).astype(jnp.float32),
        lax.psum_scatter(
            part_out.astype(jnp.bfloat16), "dp", scatter_dimension=0, tiled=True
        ).astype(jnp.float32),
    )
    grad_gate, grad_lift, grad_out = (
        lax.psum(share_gate.astype(jnp.bfloat16), "seq").astype(jnp.float32),
        lax.psum(share_lift.astype(jnp.bfloat16), "seq").astype(jnp.float32),
        lax.psum(share_out.astype(jnp.bfloat16), "seq").astype(jnp.float32),
    )
    return (d_queries[None], d_keys[None], d_values[None], grad_gate, grad_lift, grad_out)


def solution(mesh):
    in_specs = (
        P("dp", "seq", None),
        P("dp", "seq", None),
        P("dp", "seq", None),
        P("dp", "seq", None),
        P("dp", "seq", None),
        P(),
        P(),
        P("dp", "seq"),
        P("dp"),
        P("dp", None),
        P("dp", None),
        P("dp", None),
    )
    out_specs = (
        P("dp", "seq", None),
        P("dp", "seq", None),
        P("dp", "seq", None),
        P("dp", None),
        P("dp", None),
        P("dp", None),
    )
    return jax.shard_map(shards, mesh=mesh, in_specs=in_specs, out_specs=out_specs, check_vma=False)
```

profile of v0, /device:TPU:1, one launch (start us, length us, event | category | flops | bytes accessed | tf_op | source)
XLA Modules:
  0.0 702.5 jit_solution(1109292833867318314)
XLA Ops:
  13.3 12.6 %all-to-all-start = ((bf16[128,16,128]{0,2,1:T(8,128)(2,1)}), bf16[128,16,128]{0,2,1:T(8,128)(2,1)S(1)}, u32[]{:S(2)}, u32[]{:S(2)}) async-start(bf16[128,16,128]{0,2,1:T(8,128)(2,1)} %bitcast.7), calls=%async_computation | async-start | bytes 1048576 | tf_op jit(solution)/shard_map/all_to_all | solution.py:162
  26.9 20.7 %all-to-all-done = bf16[128,16,128]{0,2,1:T(8,128)(2,1)S(1)} async-done(((bf16[128,16,128]{0,2,1:T(8,128)(2,1)}), bf16[128,16,128]{0,2,1:T(8,128)(2,1)S(1)}, u32[]{:S(2)}, u32[]{:S(2)}) %all-to-all-start) | async-done | bytes 524320 | tf_op jit(solution)/shard_map/all_to_all | solution.py:162
  47.6 4.5 all-to-all-start.1
  53.1 17.1 %all-to-all-done.1 = bf16[128,16,128]{0,2,1:T(8,128)(2,1)S(1)} async-done(((bf16[128,16,128]{0,2,1:T(8,128)(2,1)}), bf16[128,16,128]{0,2,1:T(8,128)(2,1)S(1)}, u32[]{:S(2)}, u32[]{:S(2)}) %all-to-all-start.1) | async-done | bytes 524320 | tf_op jit(solution)/shard_map/all_to_all | solution.py:163
  70.2 5.5 all-to-all-start.4
  78.3 20.8 %all-to-all-done.4 = bf16[128,16,128]{0,2,1:T(8,128)(2,1)S(1)} async-done(((bf16[128,16,128]{0,2,1:T(8,128)(2,1)}), bf16[128,16,128]{0,2,1:T(8,128)(2,1)S(1)}, u32[]{:S(2)}, u32[]{:S(2)}) %all-to-all-start.4) | async-done | bytes 524320 | tf_op jit(solution)/shard_map/all_to_all | solution.py:164
  99.1 4.2 all-to-all-start.2
  106.7 6.0 all-to-all-done.2
  112.8 4.1 all-to-all-start.3
  117.7 13.1 %while.25 = (s32[]{:T(128)}, bf16[4,512,1,128]{3,1,2,0:T(8,128)(2,1)}, bf16[4,512,1,128]{3,1,2,0:T(8,128)(2,1)S(1)}, bf16[2048,1,128]{2,0,1:T(8,128)(2,1)S(1)}, bf16[2048,1,128]{2,0,1:T(8,128)(2,1)S(1)}, /*index=5*/s32[]{:T(128)}) while((s32[]{:T(128)}, bf16[4,512,1,128]{3,1,2,0:T(8,128)(2,1)}, bf16[4,512,1,128]{3,1,2,0:T(8,128)(2,1)S(1)}, ...), condition=%wide.region_10.11_spmd, body=%wide.region_7.10_spmd.sunk | while | flops 546372608 | bytes 13904457 | solution.py:70
  130.8 11.7 %all-to-all-done.3 = bf16[16,16,1536]{2,1,0:T(8,128)(2,1)S(1)} async-done(((bf16[16,16,1536]{2,1,0:T(8,128)(2,1)}), bf16[16,16,1536]{2,1,0:T(8,128)(2,1)S(1)}, u32[]{:S(2)}, u32[]{:S(2)}) %all-to-all-start.3) | async-done | bytes 786464 | tf_op jit(solution)/shard_map/all_to_all | solution.py:140
  142.5 4.9 all-to-all-start.5
  152.0 15.6 %all-to-all-done.5 = bf16[16,128,128]{2,1,0:T(8,128)(2,1)} async-done(((bf16[16,128,128]{2,1,0:T(8,128)(2,1)}), bf16[16,128,128]{2,1,0:T(8,128)(2,1)}, u32[]{:S(2)}, u32[]{:S(2)}) %all-to-all-start.5) | async-done | bytes 524320 | tf_op jit(solution)/shard_map/all_to_all | solution.py:174
  172.9 7.7 %reshape.446 = bf16[16,262144]{1,0:T(8,128)(2,1)} reshape(bf16[4194304]{0:T(1024)(128)(2,1)} %all-gather.3.cloned.1.call-done) | data formatting | bytes 16777216 | tf_op jit(solution)/shard_map/all_gather | solution.py:24
  180.5 4.7 slice.18
  189.9 4.8 reshape_reshape.18
  194.7 4.1 reshape_reshape.19
  209.7 4.2 convolution_convert_fusion.1
  214.9 4.8 all-to-all-start.6
  219.9 4.3 convolution_convert_fusion.2
  224.2 9.3 %all-to-all-done.6 = bf16[128,16,128]{2,0,1:T(8,128)(2,1)} async-done(((bf16[128,16,128]{2,0,1:T(8,128)(2,1)}), bf16[128,16,128]{2,0,1:T(8,128)(2,1)}, u32[]{:S(2)}, u32[]{:S(2)}) %all-to-all-start.6) | async-done | bytes 524320 | tf_op jit(solution)/shard_map/all_to_all | solution.py:204
  234.4 51.8 %while.26 = (s32[]{:T(128)}, f32[2048,1,128]{0,2,1:T(8,128)S(1)}, f32[2048,1,128]{0,2,1:T(8,128)S(1)}, bf16[4,512,1,128]{3,1,2,0:T(8,128)(2,1)}, bf16[4,512,1,12...) while((s32[]{:T(128)}, f32[2048,1,128]{0,2,1:T(8,128)S(1)}, ...), condition=%wide.region_18.19_spmd.clone, body=%wide.region_14.18_spmd.clone.sunk | while | flops 1365309952 | bytes 77749960 | solution.py:100
  250.9 3.7 fusion.117
  263.9 3.7 fusion.117
  276.8 3.7 fusion.117
  287.3 4.5 all-to-all-start.8
  292.1 14.2 %all-to-all-done.8 = bf16[16,128,128]{2,1,0:T(8,128)(2,1)S(1)} async-done(((bf16[16,128,128]{2,1,0:T(8,128)(2,1)}), bf16[16,128,128]{2,1,0:T(8,128)(2,1)S(1)}, u32[]{:S(2)}, u32[]{:S(2)}) %all-to-all-start.8) | async-done | bytes 524320 | tf_op jit(solution)/shard_map/all_to_all | solution.py:210
  306.3 17.9 %all_to_all.133 = bf16[16,128,128]{2,1,0:T(8,128)(2,1)S(1)} all-to-all(bf16[16,128,128]{2,1,0:T(8,128)(2,1)S(1)} %bitcast.232), channel_id=1, replica_groups=mesh['dp'=16,'seq'=16] {'seq'}, dimensions={0} | all-to-all | bytes 1048576 | tf_op jit(solution)/shard_map/all_to_all | solution.py:211
  324.2 4.5 all-to-all-start.7
  328.8 82.0 %reduce-scatter.8.cloned.1.call-done = bf16[64,1536]{1,0:T(8,128)(2,1)} async-done(((bf16[1024,1536]{1,0:T(8,128)(2,1)}), bf16[64,1536]{1,0:T(8,128)(2,1)}) %reduce-scatter.8.cloned.1.call-update) | async-done | bytes 196624 | tf_op jit(solution)/shard_map/reduce_scatter | solution.py:220
  410.8 92.8 %reduce-scatter.6.cloned.1.call-done = bf16[128,1024]{1,0:T(8,128)(2,1)} async-done(((bf16[2048,1024]{1,0:T(8,128)(2,1)}), bf16[128,1024]{1,0:T(8,128)(2,1)}) %reduce-scatter.6.cloned.1.call-update) | async-done | bytes 262160 | tf_op jit(solution)/shard_map/reduce_scatter | solution.py:217
  507.6 183.5 %all-reduce.3.cloned.1.call-done = (bf16[16,2048]{1,0:T(8,128)(2,1)}, bf16[128,1024]{1,0:T(8,128)(2,1)}, bf16[64,1536]{1,0:T(8,128)(2,1)}) async-done(((bf16[16,2048]{1,0:T(8,128)(2,1)}, bf16[128,1024]{1,0:T(8,128)(2,1)}, bf16[64,1536]{1,0:T(8,128)(2,1)}), (bf16[16,2048]{1,0:T(8,128)(2,1)}, bf16[128,1024]{1,0:T(8,128)(2,1)}, bf16[64,1536]{1,0:T(8,128)(2,1)})) %all-reduce.3.cloned.1.call-update) | async-done | bytes 524304 | tf_op jit(solution)/shard_map/psum | solution.py:225
  (164 shorter events, 105.6 us)
Async XLA Ops:
  7.2 18.8 %copy-start.8 = (bf16[1,128,2048]{2,1,0:T(8,128)(2,1)S(1)}, bf16[1,128,2048]{2,1,0:T(8,128)(2,1)}, u32[]{:S(2)}) copy-start(bf16[1,128,2048]{2,1,0:T(8,128)(2,1)} %param.17) | copy-start | bytes 1572868
  7.2 44.9 %copy-start.9 = (bf16[1,128,2048]{2,1,0:T(8,128)(2,1)S(1)}, bf16[1,128,2048]{2,1,0:T(8,128)(2,1)}, u32[]{:S(2)}) copy-start(bf16[1,128,2048]{2,1,0:T(8,128)(2,1)} %param.18) | copy-start | bytes 1572868
  7.2 45.9 %copy-start.15 = (s32[1,128]{1,0:T(1,128)S(1)}, s32[1,128]{1,0:T(1,128)}, u32[]{:S(2)}) copy-start(s32[1,128]{1,0:T(1,128)} %param.23) | copy-start | bytes 1540
  7.2 165.7 %all-gather.3.cloned.1.call-start = ((), (), s32[]{:S(2)}) async-start(), calls=%async_computation.16 | async-start | bytes 8912896 | tf_op jit(solution)/shard_map/all_gather | solution.py:24
  9.5 68.4 %copy-start.5 = (bf16[1,128,1536]{2,1,0:T(8,128)(2,1)S(1)}, bf16[1,128,1536]{2,1,0:T(8,128)(2,1)}, u32[]{:S(2)}) copy-start(bf16[1,128,1536]{2,1,0:T(8,128)(2,1)} %param.20) | copy-start | bytes 1179652
  11.2 92.2 %copy-start.13 = (f32[1536]{0:T(1024)S(1)}, f32[1536]{0:T(1024)}, u32[]{:S(2)}) copy-start(f32[1536]{0:T(1024)} %param.22) | copy-start | bytes 18436
  11.2 92.2 %copy-start.14 = (f32[1536]{0:T(1024)S(1)}, f32[1536]{0:T(1024)}, u32[]{:S(2)}) copy-start(f32[1536]{0:T(1024)} %param.21) | copy-start | bytes 18436
  13.3 34.3 %all-to-all-start = ((bf16[128,16,128]{0,2,1:T(8,128)(2,1)}), bf16[128,16,128]{0,2,1:T(8,128)(2,1)S(1)}, u32[]{:S(2)}, u32[]{:S(2)}) async-start(bf16[128,16,128]{0,2,1:T(8,128)(2,1)} %bitcast.7), calls=%async_computation | async-start | bytes 1048576 | tf_op jit(solution)/shard_map/all_to_all | solution.py:162
  47.6 22.6 %all-to-all-start.1 = ((bf16[128,16,128]{0,2,1:T(8,128)(2,1)}), bf16[128,16,128]{0,2,1:T(8,128)(2,1)S(1)}, u32[]{:S(2)}, u32[]{:S(2)}) async-start(bf16[128,16,128]{0,2,1:T(8,128)(2,1)} %bitcast.11), calls=%async_computation.1 | async-start | bytes 1048576 | tf_op jit(solution)/shard_map/all_to_all | solution.py:163
  70.2 28.9 %all-to-all-start.4 = ((bf16[128,16,128]{0,2,1:T(8,128)(2,1)}), bf16[128,16,128]{0,2,1:T(8,128)(2,1)S(1)}, u32[]{:S(2)}, u32[]{:S(2)}) async-start(bf16[128,16,128]{0,2,1:T(8,128)(2,1)} %bitcast.25), calls=%async_computation.4 | async-start | bytes 1048576 | tf_op jit(solution)/shard_map/all_to_all | solution.py:164
  99.1 13.6 %all-to-all-start.2 = ((s32[16,1,16]{2,1,0:T(1,128)}), s32[16,1,16]{2,1,0:T(1,128)S(1)}, u32[]{:S(2)}, u32[]{:S(2)}) async-start(s32[16,1,16]{2,1,0:T(1,128)} %all_to_all.105), calls=%async_computation.2 | async-start | bytes 16384 | tf_op jit(solution)/shard_map/all_to_all | solution.py:147
  112.8 29.7 %all-to-all-start.3 = ((bf16[16,16,1536]{2,1,0:T(8,128)(2,1)}), bf16[16,16,1536]{2,1,0:T(8,128)(2,1)S(1)}, u32[]{:S(2)}, u32[]{:S(2)}) async-start(bf16[16,16,1536]{2,1,0:T(8,128)(2,1)} %bitcast.22), calls=%async_computation.3 | async-start | bytes 1572864 | tf_op jit(solution)/shard_map/all_to_all | solution.py:140
  130.8 21.2 %copy-start.10 = (bf16[2048,1,128]{2,0,1:T(8,128)(2,1)}, bf16[2048,1,128]{2,0,1:T(8,128)(2,1)S(1)}, u32[]{:S(2)}) copy-start(bf16[2048,1,128]{2,0,1:T(8,128)(2,1)S(1)} %get-tuple-element.385) | copy-start | bytes 1572868
  142.5 25.0 %all-to-all-start.5 = ((bf16[16,128,128]{2,1,0:T(8,128)(2,1)}), bf16[16,128,128]{2,1,0:T(8,128)(2,1)}, u32[]{:S(2)}, u32[]{:S(2)}) async-start(bf16[16,128,128]{2,1,0:T(8,128)(2,1)} %bitcast.28), calls=%async_computation.5 | async-start | bytes 1048576 | tf_op jit(solution)/shard_map/all_to_all | solution.py:174
  147.5 181.4 %reduce-scatter.4.cloned.1.call-start = ((), (), s32[]{:S(2)}) async-start(), calls=%async_computation.13 | async-start | bytes 1114112 | tf_op jit(solution)/shard_map/reduce_scatter | solution.py:214
  180.5 6.2 copy-start.3
  194.7 5.7 copy-start.4
  198.8 4.9 copy-start.6
  198.8 4.9 copy-start.12
  209.7 201.1 %reduce-scatter.8.cloned.1.call-start = ((), (), s32[]{:S(2)}) async-start(), calls=%async_computation.15 | async-start | bytes 3342336 | tf_op jit(solution)/shard_map/reduce_scatter | solution.py:220
  214.9 18.6 %all-to-all-start.6 = ((bf16[128,16,128]{2,0,1:T(8,128)(2,1)}), bf16[128,16,128]{2,0,1:T(8,128)(2,1)}, u32[]{:S(2)}, u32[]{:S(2)}) async-start(bf16[128,16,128]{2,0,1:T(8,128)(2,1)} %bitcast.194), calls=%async_computation.6 | async-start | bytes 1048576 | tf_op jit(solution)/shard_map/all_to_all | solution.py:204
  219.6 284.0 %reduce-scatter.6.cloned.1.call-start = ((), (), s32[]{:S(2)}) async-start(), calls=%async_computation.14 | async-start | bytes 4456448 | tf_op jit(solution)/shard_map/reduce_scatter | solution.py:217
  224.2 10.2 %copy-start.7 = (f32[2048,1,128]{0,2,1:T(8,128)S(1)}, f32[2048,1,128]{0,2,1:T(8,128)}, u32[]{:S(2)}) copy-start(f32[2048,1,128]{0,2,1:T(8,128)} %custom-call.1) | copy-start | bytes 3145732
  250.9 3.7 copy-start.1
  250.9 3.7 copy-start.11
  263.9 3.7 copy-start.1
  263.9 3.7 copy-start.11
  276.8 3.7 copy-start.1
  276.8 3.7 copy-start.11
  287.3 19.0 %all-to-all-start.8 = ((bf16[16,128,128]{2,1,0:T(8,128)(2,1)}), bf16[16,128,128]{2,1,0:T(8,128)(2,1)S(1)}, u32[]{:S(2)}, u32[]{:S(2)}) async-start(bf16[16,128,128]{2,1,0:T(8,128)(2,1)} %bitcast.37), calls=%async_computation.8 | async-start | bytes 1048576 | tf_op jit(solution)/shard_map/all_to_all | solution.py:210
  324.2 182.0 %all-to-all-start.7 = ((bf16[16,128,128]{2,1,0:T(8,128)(2,1)}), bf16[16,128,128]{2,1,0:T(8,128)(2,1)S(1)}, u32[]{:S(2)}, u32[]{:S(2)}) async-start(bf16[16,128,128]{2,1,0:T(8,128)(2,1)} %bitcast.34), calls=%async_computation.7 | async-start | bytes 1048576 | tf_op jit(solution)/shard_map/all_to_all | solution.py:209
  328.8 362.3 %all-reduce.3.cloned.1.call-start = ((), (), s32[]{:S(2)}) async-start(), calls=%async_computation.17 | async-start | bytes 1048576 | tf_op jit(solution)/shard_map/psum | solution.py:225
  (9 other events, 20.9 us)
Sparse Core Ops, SparseCore 0:
  11.4 155.1 all-gather.2
  209.8 102.7 reduce-scatter.3
  315.3 95.4 reduce-scatter.7
  413.4 90.2 reduce-scatter.5
  506.6 184.4 all-reduce.2
where the time goes:
time: 704 us; the launch traced here: 703 us
  waiting for transfers between devices  474 us (67%)
  matrix products  61 us (9%)
  local copies, waits for them, and re-layouts  59.7 us (8%)
  starting transfers between devices  50.1 us (7%)
  other arithmetic  25 us (4%)
  blocking collectives  17.9 us (3%)
  between operations  14.7 us (2%)
    psum x1, waiting for transfers between devices, shards(): lax.psum(share_gate.astype(jnp.bfloat16), 'seq').astype(jnp.float32)  183 us
    reduce_scatter x1, waiting for transfers between devices, shards(): lax.psum_scatter(part_lift.astype(jnp.bfloat16), 'dp', scatter_dimension=...  92.8 us
    reduce_scatter x1, waiting for transfers between devices, shards(): lax.psum_scatter(part_out.astype(jnp.bfloat16), 'dp', scatter_dimension=0...  82 us
    all_to_all x1, waiting for transfers between devices, shards(): lax.all_to_all(value_states[0], 'seq', split_axis=1, concat_axis=0, tiled...  20.8 us
    all_to_all x1, waiting for transfers between devices, shards(): lax.all_to_all(queries[0], 'seq', split_axis=1, concat_axis=0, tiled=True)  20.7 us
    all_to_all x1, blocking collectives, shards(): lax.all_to_all(grad_value, 'seq', split_axis=0, concat_axis=1, tiled=True)  17.9 us
    all_to_all x1, waiting for transfers between devices, shards(): lax.all_to_all(key_states[0], 'seq', split_axis=1, concat_axis=0, tiled=T...  17.1 us
    all_to_all x1, waiting for transfers between devices, shards(): lax.all_to_all(mixed_heads, 'seq', split_axis=0, concat_axis=1, tiled=True)  15.6 us
  transfers between devices with their start and end apart: 14, of which 11 were waited for; matrix products, arithmetic and copies ran while one was open for 13% of the time, Pallas kernels for 0%

commit v1 on v0

v1 whole, which is shorter than its diff:
```python
import functools
import math

import jax
import jax.numpy as jnp
from jax import lax
from jax.experimental import pallas as pl
from jax.experimental.pallas import tpu as pltpu
from jax.sharding import PartitionSpec as P

HD = 128
ZD = 1536
PH = 1024
FEAT = 2048
TEMB = 256
LEN = 2048
TOK = 128
EPSILON = 1e-06
SCALE = HD ** (-0.5)
LOG2 = SCALE * math.log2(math.e)
QB = 256
KB = 256
MESH = pl.DeviceIdType.MESH
F32 = jnp.float32
BF16 = jnp.bfloat16

SCRATCH = dict(
    qh=pltpu.VMEM((LEN, HD), BF16),
    kh=pltpu.VMEM((LEN, HD), BF16),
    vh=pltpu.VMEM((LEN, HD), BF16),
    gcols=pltpu.VMEM((TEMB, HD), BF16),
    embs=pltpu.VMEM((16, 8, TEMB), F32),
    rows_send=pltpu.VMEM((256, ZD + 128), BF16),
    rows_got=pltpu.VMEM((256, ZD + 128), BF16),
    liftf=pltpu.VMEM((4, 4, 128, PH), BF16),
    outf=pltpu.VMEM((4, 4, 64, ZD), BF16),
    o32=pltpu.VMEM((LEN, HD), F32),
    lse=pltpu.VMEM((8, LEN), F32),
    gated=pltpu.VMEM((LEN, HD), BF16),
    mix_tok=pltpu.VMEM((TOK, FEAT), BF16),
    hid2=pltpu.VMEM((2 * TOK, FEAT), BF16),
    act2=pltpu.VMEM((2 * TOK, PH), BF16),
    gpf=pltpu.VMEM((2, TOK, ZD // 2), BF16),
    gp2=pltpu.VMEM((2 * TOK, ZD // 2), BF16),
    glf=pltpu.VMEM((2, TOK, PH // 2), BF16),
    gl2=pltpu.VMEM((2 * TOK, PH // 2), BF16),
    ghs=pltpu.VMEM((TOK, FEAT), BF16),
    gh=pltpu.VMEM((LEN, HD), BF16),
    do=pltpu.VMEM((LEN, HD), BF16),
    drow=pltpu.VMEM((8, LEN), F32),
    dq32=pltpu.VMEM((LEN, HD), F32),
    dqb=pltpu.VMEM((LEN, HD), BF16),
    dkb=pltpu.VMEM((LEN, HD), BF16),
    dvb=pltpu.VMEM((LEN, HD), BF16),
    ggs=pltpu.VMEM((8, HD), F32),
    ggall=pltpu.VMEM((16, 8, HD), F32),
    gfull=pltpu.VMEM((TEMB, HD), F32),
    gsl=pltpu.VMEM((16, HD), F32),
    gl_x=pltpu.VMEM((4, 4, 128, PH // 2), BF16),
    go_x=pltpu.VMEM((4, 4, 64, ZD // 2), BF16),
    rl_x=pltpu.VMEM((3, 4, 128, PH // 2), BF16),
    ro_x=pltpu.VMEM((3, 4, 64, ZD // 2), BF16),
    gl_y=pltpu.VMEM((4, 128, PH // 2), BF16),
    go_y=pltpu.VMEM((4, 64, ZD // 2), BF16),
    rl_y=pltpu.VMEM((3, 4, 32, PH // 2), BF16),
    ro_y=pltpu.VMEM((3, 4, 16, ZD // 2), BF16),
    gl_z=pltpu.VMEM((4, 32, PH // 2), BF16),
    go_z=pltpu.VMEM((4, 16, ZD // 2), BF16),
    rl_z=pltpu.VMEM((7, 32, PH // 2), BF16),
    ro_z=pltpu.VMEM((7, 16, ZD // 2), BF16),
    pl_f=pltpu.VMEM((32, PH // 2), F32),
    po_f=pltpu.VMEM((16, ZD // 2), F32),
    s_a2a=pltpu.SemaphoreType.DMA((8, 16)),
    r_a2a=pltpu.SemaphoreType.DMA((8, 16)),
    s_rel=pltpu.SemaphoreType.DMA((16,)),
    r_rel=pltpu.SemaphoreType.DMA((16,)),
    s_gate=pltpu.SemaphoreType.DMA((4, 16)),
    r_gate=pltpu.SemaphoreType.DMA((4, 16)),
    s_w=pltpu.SemaphoreType.DMA((2, 13)),
    r_w=pltpu.SemaphoreType.DMA((2, 13)),
    s_pair=pltpu.SemaphoreType.DMA((4,)),
    r_pair=pltpu.SemaphoreType.DMA((4,)),
    s_red=pltpu.SemaphoreType.DMA((2, 20)),
    r_red=pltpu.SemaphoreType.DMA((2, 20)),
    local=pltpu.SemaphoreType.DMA((20,)),
)
NAMES = list(SCRATCH)


def dot(a, b, dims, precision=None):
    return lax.dot_general(
        a, b, (dims, ((), ())), precision=precision, preferred_element_type=F32
    )


def step_kernel(*refs):
    q, k, v, res, enc, gain, bias, trow, tcol, emb, gate, lift, outw = refs[:13]
    dq, dk, dv, ggate, glift, gout = refs[13:19]
    s = dict(zip(NAMES, refs[19:]))
    dp, me = lax.axis_index("dp"), lax.axis_index("seq")
    zl, x = lax.div(dp, 4), lax.rem(dp, 4)
    zh, yc = lax.div(me, 8), lax.rem(me, 8)
    y, c = lax.div(yc, 2), lax.rem(yc, 2)
    z = zh * 4 + zl
    partner = (dp, me + 1 - 2 * c)

    def at_x(i):
        return (zl * 4 + lax.rem(x + i, 4), me)

    def at_y(i):
        return (dp, zh * 8 + lax.rem(y + i, 4) * 2 + c)

    def at_z(i):
        to = lax.rem(z + i, 8)
        return (lax.rem(to, 4) * 4 + x, lax.div(to, 4) * 8 + yc)

    def at_yc(i):
        return (dp, zh * 8 + lax.rem(yc + i, 8))

    def cols(j):
        return pl.ds(pl.multiple_of(j * 128, 128), 128)

    def remote(src, dst, send, recv, device):
        return pltpu.make_async_remote_copy(
            src_ref=src, dst_ref=dst, send_sem=send, recv_sem=recv,
            device_id=device, device_id_type=MESH,
        )

    finish = []

    def go(*copy):
        made = remote(*copy)
        made.start()
        finish.append(made.wait_send)
        return made

    barrier = pltpu.get_barrier_semaphore()

    def greet(i, _):
        pl.semaphore_signal(barrier, 1, device_id=(dp, lax.rem(me + i, 16)), device_id_type=MESH)
        pl.semaphore_signal(barrier, 1, device_id=(lax.rem(dp + i, 16), me), device_id_type=MESH)
        return 0

    lax.fori_loop(1, 16, greet, 0)
    for i in range(1, 4):
        other = (lax.rem(zl + i, 4) * 4 + x, (1 - zh) * 8 + yc)
        pl.semaphore_signal(barrier, 1, device_id=other, device_id_type=MESH)
    pl.semaphore_wait(barrier, 33)

    def tok_to_head(t, src, dst):
        def copy(j, owner):
            return remote(
                src.at[:, cols(j)], dst.at[cols(owner), :],
                s["s_a2a"].at[t, j], s["r_a2a"].at[t, owner], (dp, j),
            )

        def start(i, _):
            copy(lax.rem(me + i, 16), me).start()
            return 0

        own = pltpu.make_async_copy(src.at[:, cols(me)], dst.at[cols(me), :], s["local"].at[t])
        own.start()
        lax.fori_loop(1, 16, start, 0)

        def wait():
            def one(i, _):
                j = lax.rem(me + i, 16)
                copy(j, j).wait_recv()
                return 0

            own.wait()
            lax.fori_loop(1, 16, one, 0)

        def sent():
            def one(i, _):
                copy(lax.rem(me + i, 16), me).wait_send()
                return 0

            lax.fori_loop(1, 16, one, 0)

        finish.append(sent)
        return wait

    def head_to_tok(t, src, dst):
        def copy(j, owner):
            return remote(
                src.at[cols(j), :], dst.at[:, cols(owner)],
                s["s_a2a"].at[t, j], s["r_a2a"].at[t, owner], (dp, j),
            )

        own = pltpu.make_async_copy(src.at[cols(me), :], dst.at[:, cols(me)], s["local"].at[t])

        def send(j):
            @pl.when(j != me)
            def _():
                copy(j, me).start()

            @pl.when(j == me)
            def _():
                own.start()

        def wait():
            def one(i, _):
                j = lax.rem(me + i, 16)
                copy(j, j).wait_recv()
                return 0

            own.wait()
            lax.fori_loop(1, 16, one, 0)

        def sent():
            def one(i, _):
                copy(lax.rem(me + i, 16), me).wait_send()
                return 0

            lax.fori_loop(1, 16, one, 0)

        finish.append(sent)
        return send, wait

    def spread(t, src_of, dst_of, index, device_of):
        def copy(j, owner):
            return remote(
                src_of(j), dst_of(owner), s["s_gate"].at[t, j], s["r_gate"].at[t, owner],
                device_of(j),
            )

        def start(i, _):
            copy(lax.rem(index + i, 16), index).start()
            return 0

        own = pltpu.make_async_copy(src_of(index), dst_of(index), s["local"].at[8 + t])
        own.start()
        lax.fori_loop(1, 16, start, 0)

        def wait():
            def one(i, _):
                j = lax.rem(index + i, 16)
                copy(j, j).wait_recv()
                return 0

            own.wait()
            lax.fori_loop(1, 16, one, 0)

        def sent():
            def one(i, _):
                copy(lax.rem(index + i, 16), index).wait_send()
                return 0

            lax.fori_loop(1, 16, one, 0)

        finish.append(sent)
        return wait

    weights = [(lift, s["liftf"], 64, 256), (outw, s["outf"], 32, 384)]
    z_hops = [at_z(1), at_z(7), at_z(2 + 4 * c)]
    along_z = []
    for n, (shard, full, height, width) in enumerate(weights):
        rows = pl.ds(pl.multiple_of(c * height, height), height)
        part = pl.ds(pl.multiple_of(y * width, 128), width)
        for i, device in enumerate(z_hops):
            along_z.append(
                go(shard.at[rows, part], full.at[zl, x, rows, part],
                   s["s_w"].at[n, i], s["r_w"].at[n, i], device).wait_recv
            )
        own = pltpu.make_async_copy(
            shard.at[rows, part], full.at[zl, x, rows, part], s["local"].at[12 + n]
        )
        own.start()
        along_z.append(own.wait)
    got_q = tok_to_head(0, q, s["qh"])
    got_k = tok_to_head(1, k, s["kh"])
    got_v = tok_to_head(2, v, s["vh"])
    got_gate = spread(
        0, lambda j: gate.at[:, cols(me)],
        lambda j: s["gcols"].at[pl.ds(pl.multiple_of(j * 16, 16), 16), :], dp,
        lambda j: (j, me),
    )
    got_emb = spread(1, lambda j: emb, lambda j: s["embs"].at[j], dp, lambda j: (j, me))

    wide = enc[...].astype(F32)
    centred = wide - jnp.mean(wide, axis=-1, keepdims=True)
    variance = jnp.mean(centred * centred, axis=-1, keepdims=True)
    normed = (centred * lax.rsqrt(variance + EPSILON) * gain[...] + bias[...]).astype(BF16)
    own_row, own_col = lax.shift_right_logical(trow[...], 7), lax.shift_right_logical(tcol[...], 7)
    before = lax.broadcasted_iota(jnp.int32, (TOK, TOK), 0) < lax.broadcasted_iota(
        jnp.int32, (TOK, TOK), 1
    )
    same = jnp.where((own_col == own_row) & before, 1.0, 0.0)
    slot = own_row.astype(F32) * 16.0 + jnp.sum(same, axis=0, keepdims=True)
    place = jnp.broadcast_to(((tcol[...] & 127) + 1).astype(F32), (TOK, 128)).astype(BF16)
    slots = lax.broadcasted_iota(jnp.int32, (256, TOK), 0).astype(F32)
    pick = jnp.where(slots == slot, 1.0, 0.0).astype(BF16)
    s["rows_send"][:, :ZD] = dot(pick, normed, ((1,), (0,))).astype(BF16)
    s["rows_send"][:, ZD:] = dot(pick, place, ((1,), (0,))).astype(BF16)

    def relay(j, owner):
        return remote(
            s["rows_send"].at[pl.ds(pl.multiple_of(j * 16, 16), 16), :],
            s["rows_got"].at[pl.ds(pl.multiple_of(owner * 16, 16), 16), :],
            s["s_rel"].at[j], s["r_rel"].at[owner], (dp, j),
        )

    def relay_start(i, _):
        relay(lax.rem(me + i, 16), me).start()
        return 0

    lax.fori_loop(1, 16, relay_start, 0)
    mine = pl.ds(pl.multiple_of(me * 16, 16), 16)
    relay_own = pltpu.make_async_copy(
        s["rows_send"].at[mine, :], s["rows_got"].at[mine, :], s["local"].at[14]
    )
    relay_own.start()

    def relay_sent():
        def one(i, _):
            relay(lax.rem(me + i, 16), me).wait_send()
            return 0

        lax.fori_loop(1, 16, one, 0)

    finish.append(relay_sent)

    for wait in along_z:
        wait()
    along_y = []
    for n, (_, full, height, width) in enumerate(weights):
        rows = pl.ds(pl.multiple_of(c * height, height), height)
        part = pl.ds(pl.multiple_of(y * width, 128), width)
        for i in range(1, 4):
            piece = full.at[:, x, rows, part]
            along_y.append(
                go(piece, piece, s["s_w"].at[n, 2 + i], s["r_w"].at[n, 2 + i], at_y(i))
            )
    for copy in along_y:
        copy.wait_recv()
    along_x, to_core = [], []

    def core_piece(n, i):
        _, full, height, _ = weights[n]
        piece = full.at[:, lax.rem(x + 4 - i, 4), pl.ds(pl.multiple_of(c * height, height), height), :]
        to_core.append(go(piece, piece, s["s_w"].at[n, 9 + i], s["r_w"].at[n, 9 + i], partner))

    for n, (_, full, height, _) in enumerate(weights):
        rows = pl.ds(pl.multiple_of(c * height, height), height)
        for i in range(1, 4):
            piece = full.at[:, x, rows, :]
            along_x.append(
                (n, i, go(piece, piece, s["s_w"].at[n, 5 + i], s["r_w"].at[n, 5 + i], at_x(i)))
            )
        core_piece(n, 0)

    got_gate()
    gating = dot(emb[...].astype(BF16), s["gcols"][...], ((1,), (0,)))[0:1]
    got_q()
    got_k()
    got_v()
    send_mix, got_mix = head_to_tok(3, s["gated"], s["mix_tok"])

    def forward(i, _):
        block = lax.rem(lax.div(me, 2) + i, LEN // QB)
        at = pl.ds(pl.multiple_of(block * QB, QB), QB)
        scores = dot(s["qh"][at, :], s["kh"][...], ((1,), (1,)))
        most = jnp.max(scores, axis=1, keepdims=True)
        shifted = jnp.exp2((scores - most) * LOG2)
        total = jnp.sum(shifted, axis=1, keepdims=True)
        mixed = dot(shifted.astype(BF16), s["vh"][...], ((1,), (0,))) / total
        s["o32"][at, :] = mixed
        s["gated"][at, :] = (gating * mixed.astype(BF16).astype(F32)).astype(BF16)
        level = jnp.broadcast_to(most * LOG2 + jnp.log2(total), (QB, 128))
        s["lse"][:, at] = jnp.transpose(level)[0:8]
        send_mix(2 * block)
        send_mix(2 * block + 1)
        return 0

    lax.fori_loop(0, LEN // QB, forward, 0)
    for n, i, copy in along_x:
        copy.wait_recv()
        core_piece(n, i)

    def relay_wait(i, _):
        j = lax.rem(me + i, 16)
        relay(j, j).wait_recv()
        return 0

    relay_own.wait()
    lax.fori_loop(1, 16, relay_wait, 0)
    tokens = lax.broadcasted_iota(jnp.int32, (256, TOK), 1).astype(F32) + 1.0
    placed = jnp.where(s["rows_got"][:, ZD : ZD + 1].astype(F32) == tokens, 1.0, 0.0).astype(BF16)
    target = dot(placed, s["rows_got"][:, :ZD], ((0,), (0,)))
    target_norm = jnp.sqrt(jnp.sum(target * target, axis=1, keepdims=True) + EPSILON)

    got_mix()
    hidden = (res[...].astype(F32) + s["mix_tok"][...].astype(F32)).astype(BF16)
    s["hid2"][0:TOK, :] = hidden
    pair = [
        go(s["hid2"].at[0:TOK, :], s["hid2"].at[TOK:, :],
           s["s_pair"].at[0], s["r_pair"].at[0], partner)
    ]
    for copy in to_core:
        copy.wait_recv()
    lifted = jnp.zeros((TOK, PH), F32)
    for i in range(4):
        lifted += dot(
            s["hid2"][0:TOK, i * 512 : (i + 1) * 512],
            s["liftf"][i].reshape(512, PH), ((1,), (0,)),
        )
    sigmoid = jax.nn.sigmoid(lifted)
    s["act2"][0:TOK, :] = (lifted * sigmoid).astype(BF16)
    slope = sigmoid * (1.0 + lifted * (1.0 - sigmoid))
    pair.append(
        go(s["act2"].at[0:TOK, :], s["act2"].at[TOK:, :],
           s["s_pair"].at[1], s["r_pair"].at[1], partner)
    )
    predicted = jnp.zeros((TOK, ZD), F32)
    for i in range(4):
        predicted += dot(
            s["act2"][0:TOK, i * 256 : (i + 1) * 256],
            s["outf"][i].reshape(256, ZD), ((1,), (0,)),
        )
    pred_norm = jnp.sqrt(jnp.sum(predicted * predicted, axis=1, keepdims=True) + EPSILON)
    both = pred_norm * target_norm
    cosine = jnp.sum(predicted * target, axis=1, keepdims=True) / both
    grad_pred = (
        (-1.0 * ZD) * (target / both - cosine * predicted / (pred_norm * pred_norm))
    ).astype(BF16)
    s["gpf"][0] = grad_pred[:, : ZD // 2]
    s["gpf"][1] = grad_pred[:, ZD // 2 :]
    pair.append(
        go(s["gpf"].at[1 - c], s["gp2"].at[TOK:, :], s["s_pair"].at[2], s["r_pair"].at[2], partner)
    )
    for i in range(4):
        at = slice(i * 256, (i + 1) * 256)
        grad_act = dot(grad_pred, s["outf"][i].reshape(256, ZD), ((1,), (1,)))
        s["glf"][i // 2, :, (i % 2) * 256 : (i % 2 + 1) * 256] = (
            grad_act * slope[:, at]
        ).astype(BF16)
    pair.append(
        go(s["glf"].at[1 - c], s["gl2"].at[TOK:, :], s["s_pair"].at[3], s["r_pair"].at[3], partner)
    )
    grad_lifted = jnp.concatenate([s["glf"][0], s["glf"][1]], axis=1)
    for i in range(4):
        s["ghs"][:, i * 512 : (i + 1) * 512] = dot(
            grad_lifted, s["liftf"][i].reshape(512, PH), ((1,), (1,))
        ).astype(BF16)
    got_grad = tok_to_head(4, s["ghs"], s["gh"])

    s["gp2"][0:TOK, :] = s["gpf"][c]
    s["gl2"][0:TOK, :] = s["glf"][c]
    for copy in pair:
        copy.wait_recv()

    def lift_part(i, _):
        s["gl_x"][lax.div(i, 4), lax.rem(i, 4)] = dot(
            s["hid2"][:, cols(i)], s["gl2"][...], ((0,), (0,))
        ).astype(BF16)
        return 0

    lax.fori_loop(0, 16, lift_part, 0)

    def out_part(i, _):
        done = dot(s["act2"][:, cols(i)], s["gp2"][...], ((0,), (0,))).astype(BF16)
        first = 2 * i
        s["go_x"][lax.div(first, 4), lax.rem(first, 4)] = done[:64]
        s["go_x"][lax.div(first, 4), lax.rem(first, 4) + 1] = done[64:]
        return 0

    lax.fori_loop(0, 8, out_part, 0)
    sums = []
    for n, (part, room) in enumerate([("gl_x", "rl_x"), ("go_x", "ro_x")]):
        for i in range(1, 4):
            sums.append(
                go(s[part].at[:, lax.rem(x + i, 4)], s[room].at[i - 1],
                   s["s_red"].at[n, i - 1], s["r_red"].at[n, i - 1], at_x(i))
            )

    got_grad()
    ones = jnp.ones((8, HD), F32)

    def prepare(i, total):
        at = pl.ds(pl.multiple_of(i * QB, QB), QB)
        grad = s["gh"][at, :].astype(F32)
        mixed = s["o32"][at, :]
        scaled = (gating * grad).astype(BF16)
        s["do"][at, :] = scaled
        s["drow"][:, at] = dot(
            ones, scaled.astype(F32) * mixed, ((1,), (1,)), lax.Precision.HIGHEST
        )
        product = grad * mixed.astype(BF16).astype(F32)
        return total + jnp.sum(product.reshape(QB // 8, 8, HD), axis=0)

    s["ggs"][...] = lax.fori_loop(0, LEN // QB, prepare, jnp.zeros((8, HD), F32))
    got_gg = spread(2, lambda j: s["ggs"], lambda j: s["ggall"].at[j], dp, lambda j: (j, me))
    s["dq32"][...] = jnp.zeros((LEN, HD), F32)
    send_dk, got_dk = head_to_tok(5, s["dkb"], dk)
    send_dv, got_dv = head_to_tok(6, s["dvb"], dv)
    send_dq, got_dq = head_to_tok(7, s["dqb"], dq)

    def backward(i, _):
        block = lax.rem(lax.div(me, 2) + i, LEN // KB)
        at = pl.ds(pl.multiple_of(block * KB, KB), KB)
        keys = s["kh"][at, :]
        scores = dot(keys, s["qh"][...], ((1,), (1,)))
        chances = jnp.exp2(scores * LOG2 - s["lse"][0:1, :])
        s["dvb"][at, :] = dot(chances.astype(BF16), s["do"][...], ((1,), (0,))).astype(BF16)
        grad_chances = dot(s["vh"][at, :], s["do"][...], ((1,), (1,)))
        grad_scores = (chances * (grad_chances - s["drow"][0:1, :])).astype(BF16)
        s["dkb"][at, :] = (dot(grad_scores, s["qh"][...], ((1,), (0,))) * SCALE).astype(BF16)
        for send in (send_dv, send_dk):
            send(2 * block)
            send(2 * block + 1)
        s["dq32"][...] += dot(grad_scores, keys, ((0,), (0,)))
        return 0

    lax.fori_loop(0, LEN // KB, backward, 0)
    s["dqb"][...] = (s["dq32"][...] * SCALE).astype(BF16)

    def send_queries(i, _):
        send_dq(lax.rem(me + i, 16))
        return 0

    lax.fori_loop(0, 16, send_queries, 0)

    got_emb()
    got_gg()
    s["gfull"][...] = dot(
        s["embs"][...].reshape(128, TEMB), s["ggall"][...].reshape(128, HD), ((0,), (0,)),
        lax.Precision.HIGHEST,
    )
    s["gsl"][...] = s["gfull"][pl.ds(pl.multiple_of(dp * 16, 16), 16), :]
    got_ggate = spread(
        3, lambda j: s["gsl"], lambda j: ggate.at[:, cols(j)], me, lambda j: (dp, j)
    )

    for copy in sums:
        copy.wait_recv()
    s["gl_y"][...] = (s["gl_x"][:, x].astype(F32) + s["rl_x"][0].astype(F32)
                      + s["rl_x"][1].astype(F32) + s["rl_x"][2].astype(F32)).astype(BF16)
    s["go_y"][...] = (s["go_x"][:, x].astype(F32) + s["ro_x"][0].astype(F32)
                      + s["ro_x"][1].astype(F32) + s["ro_x"][2].astype(F32)).astype(BF16)
    sums = []
    reduced = [("gl_y", "rl_y", 32), ("go_y", "ro_y", 16)]
    for n, (part, room, height) in enumerate(reduced):
        for i in range(1, 4):
            rows = pl.ds(pl.multiple_of(lax.rem(y + i, 4) * height, height), height)
            sums.append(
                go(s[part].at[:, rows, :], s[room].at[i - 1],
                   s["s_red"].at[n, 2 + i], s["r_red"].at[n, 2 + i], at_y(i))
            )
    for copy in sums:
        copy.wait_recv()
    for (part, room, height), nxt in zip(reduced, ("gl_z", "go_z")):
        rows = pl.ds(pl.multiple_of(y * height, height), height)
        s[nxt][...] = (s[part][:, rows, :].astype(F32) + s[room][0].astype(F32)
                       + s[room][1].astype(F32) + s[room][2].astype(F32)).astype(BF16)
    sums = []
    for n, (part, room) in enumerate([("gl_z", "rl_z"), ("go_z", "ro_z")]):
        for i in range(1, 8):
            sums.append(
                go(s[part].at[lax.rem(z + i, 4)], s[room].at[i - 1],
                   s["s_red"].at[n, 5 + i], s["r_red"].at[n, 5 + i], at_z(i))
            )
    for copy in sums:
        copy.wait_recv()
    sums = []
    final = [
        ("gl_z", "rl_z", "pl_f", glift, 32, PH // 2),
        ("go_z", "ro_z", "po_f", gout, 16, ZD // 2),
    ]
    for n, (part, room, piece, whole, height, width) in enumerate(final):
        total = s[part][zl].astype(F32)
        for i in range(7):
            total += s[room][i].astype(F32)
        s[piece][...] = total
        to = whole.at[
            pl.ds(pl.multiple_of(y * height, height), height),
            pl.ds(pl.multiple_of(c * width, 128), width),
        ]
        own = pltpu.make_async_copy(s[piece], to, s["local"].at[15 + n])
        own.start()
        finish.append(own.wait)
        for i in range(1, 8):
            sums.append(
                go(s[piece], to, s["s_red"].at[n, 12 + i], s["r_red"].at[n, 12 + i], at_yc(i))
            )
    got_ggate()
    for copy in sums:
        copy.wait_recv()
    got_dk()
    got_dv()
    got_dq()
    for wait in finish:
        wait()


def embed_time(timestep):
    half_width = TEMB // 2
    frequency = jnp.exp(-math.log(10000.0) * jnp.arange(half_width).astype(F32) / half_width)
    angles = timestep.astype(F32)[:, None] * frequency[None, :]
    return jnp.concatenate([jnp.cos(angles), jnp.sin(angles)], axis=1).astype(BF16)


def shards(
    queries,
    key_states,
    value_states,
    residual,
    enc_hidden,
    enc_gain,
    enc_bias,
    feature_target,
    timestep,
    gate_weight,
    lift_weight,
    out_weight,
):
    embedded = jnp.broadcast_to(embed_time(timestep).astype(F32), (8, TEMB))
    anywhere = pl.BlockSpec(memory_space=pl.ANY)
    near = pl.BlockSpec(memory_space=pltpu.VMEM)
    tok = jax.ShapeDtypeStruct((TOK, FEAT), BF16)
    outs = pl.pallas_call(
        step_kernel,
        out_shape=(
            tok, tok, tok,
            jax.ShapeDtypeStruct((16, FEAT), F32),
            jax.ShapeDtypeStruct((128, PH), F32),
            jax.ShapeDtypeStruct((64, ZD), F32),
        ),
        in_specs=[anywhere] * 3 + [near] * 7 + [anywhere] * 3,
        out_specs=(anywhere,) * 6,
        scratch_shapes=list(SCRATCH.values()),
        compiler_params=pltpu.CompilerParams(
            collective_id=0, has_side_effects=True, vmem_limit_bytes=60 << 20
        ),
        name="repa_step",
    )(
        queries[0], key_states[0], value_states[0], residual[0], enc_hidden[0],
        enc_gain[None], enc_bias[None], feature_target, feature_target.reshape(TOK, 1),
        embedded, gate_weight, lift_weight, out_weight,
    )
    d_queries, d_keys, d_values, grad_gate, grad_lift, grad_out = outs
    return (d_queries[None], d_keys[None], d_values[None], grad_gate, grad_lift, grad_out)


def solution(mesh):
    tokens = P("dp", "seq", None)
    rows = P("dp", None)
    in_specs = (tokens,) * 5 + (P(), P(), P("dp", "seq"), P("dp"), rows, rows, rows)
    out_specs = (tokens,) * 3 + (rows,) * 3
    return jax.shard_map(
        shards, mesh=mesh, in_specs=in_specs, out_specs=out_specs, check_vma=False
    )
```

time: 704 us -> 202 us (0.29)
  waiting for transfers between devices: 474 us -> 0 us
  Pallas kernels: 0 us -> 190 us
  matrix products: 61 us -> 0 us
  starting transfers between devices: 50.1 us -> 0 us
  local copies, waits for them, and re-layouts: 59.7 us -> 9.97 us
  other arithmetic: 25 us -> 0.06 us
  blocking collectives: 17.9 us -> 0 us
  between operations: 14.7 us -> 1.33 us
    pallas_call x0 -> x1, Pallas kernels: none -> 190 us  [shards(): pl.pallas_call(step_kernel, out_shape=(tok, tok, tok, jax.ShapeDtypeStruc...]
    psum x1 -> x0, waiting for transfers between devices: 183 us -> none  [shards(): lax.psum(share_gate.astype(jnp.bfloat16), 'seq').astype(jnp.float32)]
    reduce_scatter x3 -> x0, waiting for transfers between devices: 175 us -> none  [the longest x1 92.8 us: shards(): lax.psum_scatter(part_lift.astype(jnp.bfloat16), 'dp', scatter_dimension=...]
    all_to_all x9 -> x0, waiting for transfers between devices: 115 us -> none  [the longest x1 20.8 us: shards(): lax.all_to_all(value_states[0], 'seq', split_axis=1, concat_axis=0, tiled...]
    dot_general x35 -> x0, matrix products: 61 us -> none  [the longest x4 14.6 us: one_block(): jnp.einsum('hbl,bhd->lhd', chances.astype(jnp.bfloat16), grad_block, pref...]
    all_to_all x9 -> x0, starting transfers between devices: 49.7 us -> none  [the longest x1 12.6 us: shards(): lax.all_to_all(queries[0], 'seq', split_axis=1, concat_axis=0, tiled=True)]
    all_to_all x1 -> x0, blocking collectives: 17.9 us -> none  [shards(): lax.all_to_all(grad_value, 'seq', split_axis=0, concat_axis=1, tiled=True)]
    convert_element_type x11 -> x1, other arithmetic: 12.4 us -> 0.01 us  [shards(): embedded = jnp.broadcast_to(embed_time(timestep).astype(F32), (8, TEMB))]
  transfers between devices with their start and end apart: 14 -> 0, of which waited for: 11 -> 0; matrix products, arithmetic and copies ran while one was open for 13% -> 0% of each run, Pallas kernels for 0% -> 0%
where the time goes in v1:
time: 202 us; the launch traced here: 201 us
  Pallas kernels  190 us (94%)
  local copies, waits for them, and re-layouts  9.97 us (5%)
    pallas_call x1, Pallas kernels, shards(): pl.pallas_call(step_kernel, out_shape=(tok, tok, tok, jax.ShapeDtypeStruc...  190 us
    unnamed x22, local copies, waits for them, and re-layouts  7.43 us

profile of v1, /device:TPU:1, one launch (start us, length us, event | category | flops | bytes accessed | tf_op | source)
XLA Modules:
  0.0 201.5 jit_solution(10470772317824051282)
XLA Ops:
  1.3 0.0 copy-start.5
  1.3 0.0 copy-start.6
  1.4 0.6 copy-done.5
  2.0 0.6 broadcast_in_dim.22.refs_5_
  2.6 0.0 copy-done.6
  2.6 0.6 broadcast_in_dim.23.refs_6_
  3.2 0.0 copy-start.7
  3.2 0.6 broadcast_in_dim.24.refs_9_
  3.8 0.1 copy-done.7
  3.8 0.7 copy.18.refs_8_
  4.6 190.1 %repa_step.1 = (bf16[128,2048]{1,0:T(8,128)(2,1)}, bf16[128,2048]{1,0:T(8,128)(2,1)}, bf16[128,2048]{1,0:T(8,128)(2,1)}, f32[16,2048]{1,0:T(8,128)}, f32[128,1024]{1,0:T(8,128)}, /*index=5*/f32[64,1536]{1,0:T(8,128)}) custom-call(bf16[128,2048]{1,0:T(8,128)(2,1)} %bitcast.10, bf16[128,2048]{1,0:T(8,128)(2,1)} %bitcast.11, bf16[128,2048]{1,0:T(8,128)(2,1)} %bitcast.12, ...), custom_call_target="tpu_custom_call" | custom-call | tf_op jit(solution)/shard_map/repa_step/pallas_call | solution.py:621
  194.7 0.0 copy-start.2
  194.7 1.9 copy.26
  196.6 0.0 copy-done.2
  196.6 0.0 copy-start.1
  196.6 0.8 copy.27
  197.4 0.4 copy-done.1
  197.9 0.0 copy-start.4
  197.9 0.0 copy-start
  197.9 0.8 copy.28
  198.7 0.2 copy-done.4
  198.9 0.7 copy.29
  199.5 0.0 copy-done
  199.5 0.0 copy-start.3
  199.5 0.8 copy.30
  200.3 0.4 copy-done.3
  200.7 0.7 copy.31
  (2 shorter events, 0.1 us)
Async XLA Ops:
  1.3 0.7 copy-start.5
  1.3 1.2 copy-start.6
  3.2 0.7 copy-start.7
  194.7 2.0 copy-start.2
  196.6 1.2 copy-start.1
  197.9 1.0 copy-start.4
  197.9 1.7 copy-start
  199.5 1.2 copy-start.3

commit v2 on v1

--- a/solution.py
+++ b/solution.py
@@ -29,6 +29,7 @@
     kh=pltpu.VMEM((LEN, HD), BF16),
     vh=pltpu.VMEM((LEN, HD), BF16),
     gcols=pltpu.VMEM((TEMB, HD), BF16),
+    emb=pltpu.VMEM((8, TEMB), F32),
     embs=pltpu.VMEM((16, 8, TEMB), F32),
     rows_send=pltpu.VMEM((256, ZD + 128), BF16),
     rows_got=pltpu.VMEM((256, ZD + 128), BF16),
@@ -59,11 +60,11 @@
     gl_x=pltpu.VMEM((4, 4, 128, PH // 2), BF16),
     go_x=pltpu.VMEM((4, 4, 64, ZD // 2), BF16),
     rl_x=pltpu.VMEM((3, 4, 128, PH // 2), BF16),
-    ro_x=pltpu.VMEM((3, 4, 64, ZD // 2), BF16),
+    ro_y=pltpu.VMEM((3, 4, 4, 16, ZD // 2), BF16),
     gl_y=pltpu.VMEM((4, 128, PH // 2), BF16),
-    go_y=pltpu.VMEM((4, 64, ZD // 2), BF16),
+    go_y=pltpu.VMEM((4, 4, 16, ZD // 2), BF16),
     rl_y=pltpu.VMEM((3, 4, 32, PH // 2), BF16),
-    ro_y=pltpu.VMEM((3, 4, 16, ZD // 2), BF16),
+    ro_x=pltpu.VMEM((3, 4, 16, ZD // 2), BF16),
     gl_z=pltpu.VMEM((4, 32, PH // 2), BF16),
     go_z=pltpu.VMEM((4, 16, ZD // 2), BF16),
     rl_z=pltpu.VMEM((7, 32, PH // 2), BF16),
@@ -94,9 +95,9 @@
 
 
 def step_kernel(*refs):
-    q, k, v, res, enc, gain, bias, trow, tcol, emb, gate, lift, outw = refs[:13]
-    dq, dk, dv, ggate, glift, gout = refs[13:19]
-    s = dict(zip(NAMES, refs[19:]))
+    q, k, v, res, enc, gain, bias, trow, when, gate, lift, outw = refs[:12]
+    dq, dk, dv, ggate, glift, gout = refs[12:18]
+    s = dict(zip(NAMES, refs[18:]))
     dp, me = lax.axis_index("dp"), lax.axis_index("seq")
     zl, x = lax.div(dp, 4), lax.rem(dp, 4)
     zh, yc = lax.div(me, 8), lax.rem(me, 8)
@@ -133,6 +134,12 @@
         made.start()
         finish.append(made.wait_send)
         return made
+
+    half = TEMB // 2
+    index = lax.broadcasted_iota(jnp.int32, (8, half), 1).astype(F32)
+    angles = when[0].astype(F32) * jnp.exp(-math.log(10000.0) * index / half)
+    s["emb"][:, :half] = jnp.cos(angles).astype(BF16).astype(F32)
+    s["emb"][:, half:] = jnp.sin(angles).astype(BF16).astype(F32)
 
     barrier = pltpu.get_barrier_semaphore()
 
@@ -276,19 +283,20 @@
         lambda j: s["gcols"].at[pl.ds(pl.multiple_of(j * 16, 16), 16), :], dp,
         lambda j: (j, me),
     )
-    got_emb = spread(1, lambda j: emb, lambda j: s["embs"].at[j], dp, lambda j: (j, me))
+    got_emb = spread(1, lambda j: s["emb"], lambda j: s["embs"].at[j], dp, lambda j: (j, me))
 
     wide = enc[...].astype(F32)
     centred = wide - jnp.mean(wide, axis=-1, keepdims=True)
     variance = jnp.mean(centred * centred, axis=-1, keepdims=True)
-    normed = (centred * lax.rsqrt(variance + EPSILON) * gain[...] + bias[...]).astype(BF16)
-    own_row, own_col = lax.shift_right_logical(trow[...], 7), lax.shift_right_logical(tcol[...], 7)
+    normed = (centred * lax.rsqrt(variance + EPSILON) * gain[...][None] + bias[...][None]).astype(BF16)
+    tcol = jnp.transpose(jnp.broadcast_to(trow[...], (TOK, TOK)))
+    own_row, own_col = lax.shift_right_logical(trow[...], 7), lax.shift_right_logical(tcol, 7)
     before = lax.broadcasted_iota(jnp.int32, (TOK, TOK), 0) < lax.broadcasted_iota(
         jnp.int32, (TOK, TOK), 1
     )
     same = jnp.where((own_col == own_row) & before, 1.0, 0.0)
     slot = own_row.astype(F32) * 16.0 + jnp.sum(same, axis=0, keepdims=True)
-    place = jnp.broadcast_to(((tcol[...] & 127) + 1).astype(F32), (TOK, 128)).astype(BF16)
+    place = ((tcol & 127) + 1).astype(F32).astype(BF16)
     slots = lax.broadcasted_iota(jnp.int32, (256, TOK), 0).astype(F32)
     pick = jnp.where(slots == slot, 1.0, 0.0).astype(BF16)
     s["rows_send"][:, :ZD] = dot(pick, normed, ((1,), (0,))).astype(BF16)
@@ -304,13 +312,6 @@
     def relay_start(i, _):
         relay(lax.rem(me + i, 16), me).start()
         return 0
-
-    lax.fori_loop(1, 16, relay_start, 0)
-    mine = pl.ds(pl.multiple_of(me * 16, 16), 16)
-    relay_own = pltpu.make_async_copy(
-        s["rows_send"].at[mine, :], s["rows_got"].at[mine, :], s["local"].at[14]
-    )
-    relay_own.start()
 
     def relay_sent():
         def one(i, _):
@@ -351,10 +352,17 @@
         core_piece(n, 0)
 
     got_gate()
-    gating = dot(emb[...].astype(BF16), s["gcols"][...], ((1,), (0,)))[0:1]
+    gating = dot(s["emb"][...].astype(BF16), s["gcols"][...], ((1,), (0,)))[0:1]
     got_q()
     got_k()
     got_v()
+    lax.fori_loop(1, 16, relay_start, 0)
+    mine = pl.ds(pl.multiple_of(me * 16, 16), 16)
+    relay_own = pltpu.make_async_copy(
+        s["rows_send"].at[mine, :], s["rows_got"].at[mine, :], s["local"].at[14]
+    )
+    relay_own.start()
+
     send_mix, got_mix = head_to_tok(3, s["gated"], s["mix_tok"])
 
     def forward(i, _):
@@ -363,11 +371,11 @@
         scores = dot(s["qh"][at, :], s["kh"][...], ((1,), (1,)))
         most = jnp.max(scores, axis=1, keepdims=True)
         shifted = jnp.exp2((scores - most) * LOG2)
-        total = jnp.sum(shifted, axis=1, keepdims=True)
-        mixed = dot(shifted.astype(BF16), s["vh"][...], ((1,), (0,))) / total
+        weight = jnp.sum(shifted, axis=1, keepdims=True)
+        mixed = dot(shifted.astype(BF16), s["vh"][...], ((1,), (0,))) / weight
         s["o32"][at, :] = mixed
         s["gated"][at, :] = (gating * mixed.astype(BF16).astype(F32)).astype(BF16)
-        level = jnp.broadcast_to(most * LOG2 + jnp.log2(total), (QB, 128))
+        level = jnp.broadcast_to(most * LOG2 + jnp.log2(weight), (QB, 128))
         s["lse"][:, at] = jnp.transpose(level)[0:8]
         send_mix(2 * block)
         send_mix(2 * block + 1)
@@ -467,17 +475,27 @@
 
     lax.fori_loop(0, 8, out_part, 0)
     sums = []
-    for n, (part, room) in enumerate([("gl_x", "rl_x"), ("go_x", "ro_x")]):
-        for i in range(1, 4):
-            sums.append(
-                go(s[part].at[:, lax.rem(x + i, 4)], s[room].at[i - 1],
-                   s["s_red"].at[n, i - 1], s["r_red"].at[n, i - 1], at_x(i))
-            )
+    for i in range(1, 4):
+        rows = pl.ds(pl.multiple_of(lax.rem(y + i, 4) * 16, 16), 16)
+        sums.append(
+            go(s["gl_x"].at[:, lax.rem(x + i, 4)], s["rl_x"].at[i - 1],
+               s["s_red"].at[0, i - 1], s["r_red"].at[0, i - 1], at_x(i))
+        )
+        sums.append(
+            go(s["go_x"].at[:, :, rows, :], s["ro_y"].at[i - 1],
+               s["s_red"].at[1, i - 1], s["r_red"].at[1, i - 1], at_y(i))
+        )
+
+    def total(own, room):
+        added = own.astype(F32)
+        for i in range(room.shape[0]):
+            added += room[i].astype(F32)
+        return added
 
     got_grad()
     ones = jnp.ones((8, HD), F32)
 
-    def prepare(i, total):
+    def prepare(i, partial):
         at = pl.ds(pl.multiple_of(i * QB, QB), QB)
         grad = s["gh"][at, :].astype(F32)
         mixed = s["o32"][at, :]
@@ -487,7 +505,7 @@
             ones, scaled.astype(F32) * mixed, ((1,), (1,)), lax.Precision.HIGHEST
         )
         product = grad * mixed.astype(BF16).astype(F32)
-        return total + jnp.sum(product.reshape(QB // 8, 8, HD), axis=0)
+        return partial + jnp.sum(product.reshape(QB // 8, 8, HD), axis=0)
 
     s["ggs"][...] = lax.fori_loop(0, LEN // QB, prepare, jnp.zeros((8, HD), F32))
     got_gg = spread(2, lambda j: s["ggs"], lambda j: s["ggall"].at[j], dp, lambda j: (j, me))
@@ -512,7 +530,25 @@
         s["dq32"][...] += dot(grad_scores, keys, ((0,), (0,)))
         return 0
 
-    lax.fori_loop(0, LEN // KB, backward, 0)
+    lax.fori_loop(0, LEN // KB // 2, backward, 0)
+
+    for copy in sums:
+        copy.wait_recv()
+    s["gl_y"][...] = total(s["gl_x"][:, x], s["rl_x"]).astype(BF16)
+    y_rows = pl.ds(pl.multiple_of(y * 16, 16), 16)
+    s["go_y"][...] = total(s["go_x"][:, :, y_rows, :], s["ro_y"]).astype(BF16)
+    sums = []
+    for i in range(1, 4):
+        rows = pl.ds(pl.multiple_of(lax.rem(y + i, 4) * 32, 32), 32)
+        sums.append(
+            go(s["gl_y"].at[:, rows, :], s["rl_y"].at[i - 1],
+               s["s_red"].at[0, 2 + i], s["r_red"].at[0, 2 + i], at_y(i))
+        )
+        sums.append(
+            go(s["go_y"].at[:, lax.rem(x + i, 4)], s["ro_x"].at[i - 1],
+               s["s_red"].at[1, 2 + i], s["r_red"].at[1, 2 + i], at_x(i))
+        )
+    lax.fori_loop(LEN // KB // 2, LEN // KB, backward, 0)
     s["dqb"][...] = (s["dq32"][...] * SCALE).astype(BF16)
 
     def send_queries(i, _):
@@ -521,38 +557,11 @@
 
     lax.fori_loop(0, 16, send_queries, 0)
 
-    got_emb()
-    got_gg()
-    s["gfull"][...] = dot(
-        s["embs"][...].reshape(128, TEMB), s["ggall"][...].reshape(128, HD), ((0,), (0,)),
-        lax.Precision.HIGHEST,
-    )
-    s["gsl"][...] = s["gfull"][pl.ds(pl.multiple_of(dp * 16, 16), 16), :]
-    got_ggate = spread(
-        3, lambda j: s["gsl"], lambda j: ggate.at[:, cols(j)], me, lambda j: (dp, j)
-    )
-
     for copy in sums:
         copy.wait_recv()
-    s["gl_y"][...] = (s["gl_x"][:, x].astype(F32) + s["rl_x"][0].astype(F32)
-                      + s["rl_x"][1].astype(F32) + s["rl_x"][2].astype(F32)).astype(BF16)
-    s["go_y"][...] = (s["go_x"][:, x].astype(F32) + s["ro_x"][0].astype(F32)
-                      + s["ro_x"][1].astype(F32) + s["ro_x"][2].astype(F32)).astype(BF16)
-    sums = []
-    reduced = [("gl_y", "rl_y", 32), ("go_y", "ro_y", 16)]
-    for n, (part, room, height) in enumerate(reduced):
-        for i in range(1, 4):
-            rows = pl.ds(pl.multiple_of(lax.rem(y + i, 4) * height, height), height)
-            sums.append(
-                go(s[part].at[:, rows, :], s[room].at[i - 1],
-                   s["s_red"].at[n, 2 + i], s["r_red"].at[n, 2 + i], at_y(i))
-            )
-    for copy in sums:
-        copy.wait_recv()
-    for (part, room, height), nxt in zip(reduced, ("gl_z", "go_z")):
-        rows = pl.ds(pl.multiple_of(y * height, height), height)
-        s[nxt][...] = (s[part][:, rows, :].astype(F32) + s[room][0].astype(F32)
-                       + s[room][1].astype(F32) + s[room][2].astype(F32)).astype(BF16)
+    y_rows = pl.ds(pl.multiple_of(y * 32, 32), 32)
+    s["gl_z"][...] = total(s["gl_y"][:, y_rows, :], s["rl_y"]).astype(BF16)
+    s["go_z"][...] = total(s["go_y"][:, x], s["ro_x"]).astype(BF16)
     sums = []
     for n, (part, room) in enumerate([("gl_z", "rl_z"), ("go_z", "ro_z")]):
         for i in range(1, 8):
@@ -560,6 +569,18 @@
                 go(s[part].at[lax.rem(z + i, 4)], s[room].at[i - 1],
                    s["s_red"].at[n, 5 + i], s["r_red"].at[n, 5 + i], at_z(i))
             )
+
+    got_emb()
+    got_gg()
+    s["gfull"][...] = dot(
+        s["embs"][...].reshape(128, TEMB), s["ggall"][...].reshape(128, HD), ((0,), (0,)),
+        lax.Precision.HIGHEST,
+    )
+    s["gsl"][...] = s["gfull"][pl.ds(pl.multiple_of(dp * 16, 16), 16), :]
+    got_ggate = spread(
+        3, lambda j: s["gsl"], lambda j: ggate.at[:, cols(j)], me, lambda j: (dp, j)
+    )
+
     for copy in sums:
         copy.wait_recv()
     sums = []
@@ -568,10 +589,7 @@
         ("go_z", "ro_z", "po_f", gout, 16, ZD // 2),
     ]
     for n, (part, room, piece, whole, height, width) in enumerate(final):
-        total = s[part][zl].astype(F32)
-        for i in range(7):
-            total += s[room][i].astype(F32)
-        s[piece][...] = total
+        s[piece][...] = total(s[part][zl], s[room])
         to = whole.at[
             pl.ds(pl.multiple_of(y * height, height), height),
             pl.ds(pl.multiple_of(c * width, 128), width),
@@ -593,11 +611,15 @@
         wait()
 
 
-def embed_time(timestep):
-    half_width = TEMB // 2
-    frequency = jnp.exp(-math.log(10000.0) * jnp.arange(half_width).astype(F32) / half_width)
-    angles = timestep.astype(F32)[:, None] * frequency[None, :]
-    return jnp.concatenate([jnp.cos(angles), jnp.sin(angles)], axis=1).astype(BF16)
+def copy_kernel(*refs):
+    sems = refs[-1]
+    copies = [
+        pltpu.make_async_copy(refs[i], refs[6 + i], sems.at[i]) for i in range(6)
+    ]
+    for copy in copies:
+        copy.start()
+    for copy in copies:
+        copy.wait()
 
 
 def shards(
@@ -614,19 +636,20 @@
     lift_weight,
     out_weight,
 ):
-    embedded = jnp.broadcast_to(embed_time(timestep).astype(F32), (8, TEMB))
     anywhere = pl.BlockSpec(memory_space=pl.ANY)
     near = pl.BlockSpec(memory_space=pltpu.VMEM)
     tok = jax.ShapeDtypeStruct((TOK, FEAT), BF16)
+    out_shape = (
+        tok, tok, tok,
+        jax.ShapeDtypeStruct((16, FEAT), F32),
+        jax.ShapeDtypeStruct((128, PH), F32),
+        jax.ShapeDtypeStruct((64, ZD), F32),
+    )
     outs = pl.pallas_call(
         step_kernel,
-        out_shape=(
-            tok, tok, tok,
-            jax.ShapeDtypeStruct((16, FEAT), F32),
-            jax.ShapeDtypeStruct((128, PH), F32),
-            jax.ShapeDtypeStruct((64, ZD), F32),
-        ),
-        in_specs=[anywhere] * 3 + [near] * 7 + [anywhere] * 3,
+        out_shape=out_shape,
+        in_specs=[anywhere] * 3 + [near] * 5 + [pl.BlockSpec(memory_space=pltpu.SMEM)]
+        + [anywhere] * 3,
         out_specs=(anywhere,) * 6,
         scratch_shapes=list(SCRATCH.values()),
         compiler_params=pltpu.CompilerParams(
@@ -635,10 +658,16 @@
         name="repa_step",
     )(
         queries[0], key_states[0], value_states[0], residual[0], enc_hidden[0],
-        enc_gain[None], enc_bias[None], feature_target, feature_target.reshape(TOK, 1),
-        embedded, gate_weight, lift_weight, out_weight,
-    )
-    d_queries, d_keys, d_values, grad_gate, grad_lift, grad_out = outs
+        enc_gain, enc_bias, feature_target, timestep, gate_weight, lift_weight, out_weight,
+    )
+    d_queries, d_keys, d_values, grad_gate, grad_lift, grad_out = pl.pallas_call(
+        copy_kernel,
+        out_shape=out_shape,
+        in_specs=[anywhere] * 6,
+        out_specs=(anywhere,) * 6,
+        scratch_shapes=[pltpu.SemaphoreType.DMA((6,))],
+        name="hand_out",
+    )(*outs)
     return (d_queries[None], d_keys[None], d_values[None], grad_gate, grad_lift, grad_out)
 
 

time: 202 us -> 274 us (1.36); the launches traced: 201 us -> 270 us
  Pallas kernels: 190 us -> 268 us
  local copies, waits for them, and re-layouts: 9.97 us -> 0 us
    pallas_call x1 -> x2, Pallas kernels: 190 us -> 268 us  [the longest x1 188 us: shards(): pl.pallas_call(step_kernel, out_shape=out_shape, in_specs=[anywhere] * 3...]
    unnamed x22 -> x0, local copies, waits for them, and re-layouts: 7.43 us -> none
where the time goes in v2:
time: 274 us; the launch traced here: 270 us
  Pallas kernels  268 us (98%)
    pallas_call x1, Pallas kernels, shards(): pl.pallas_call(step_kernel, out_shape=out_shape, in_specs=[anywhere] * 3...  188 us
    pallas_call x1, Pallas kernels, shards(): pl.pallas_call(copy_kernel, out_shape=out_shape, in_specs=[anywhere] * 6,...  80.6 us

profile of v2, /device:TPU:1, one launch (start us, length us, event | category | flops | bytes accessed | tf_op | source)
XLA Modules:
  0.0 269.7 jit_solution(5274436644810833936)
XLA Ops:
  1.3 187.9 %repa_step.1 = (bf16[128,2048]{1,0:T(8,128)(2,1)}, bf16[128,2048]{1,0:T(8,128)(2,1)}, bf16[128,2048]{1,0:T(8,128)(2,1)}, f32[16,2048]{1,0:T(8,128)}, f32[128,1024]{1,0:T(8,128)}, /*index=5*/f32[64,1536]{1,0:T(8,128)}) custom-call(bf16[128,2048]{1,0:T(8,128)(2,1)} %bitcast.8, bf16[128,2048]{1,0:T(8,128)(2,1)} %bitcast.9, bf16[128,2048]{1,0:T(8,128)(2,1)} %bitcast.10, ...), custom_call_target="tpu_custom_call" | custom-call | tf_op jit(solution)/shard_map/repa_step/pallas_call | solution.py:648
  189.2 80.6 %hand_out.1 = (bf16[128,2048]{1,0:T(8,128)(2,1)}, bf16[128,2048]{1,0:T(8,128)(2,1)}, bf16[128,2048]{1,0:T(8,128)(2,1)}, f32[16,2048]{1,0:T(8,128)}, f32[128,1024]{1,0:T(8,128)}, /*index=5*/f32[64,1536]{1,0:T(8,128)}) custom-call(bf16[128,2048]{1,0:T(8,128)(2,1)} %get-tuple-element.18.refs_0_, bf16[128,2048]{1,0:T(8,128)(2,1)} %get-tuple-element.19.refs_1_, ...), custom_call_target="tpu_custom_call" | custom-call | tf_op jit(solution)/shard_map/hand_out/pallas_call | solution.py:663

commit v3 on v2

--- a/solution.py
+++ b/solution.py
@@ -20,6 +20,7 @@
 LOG2 = SCALE * math.log2(math.e)
 QB = 256
 KB = 256
+EARLY = 6
 MESH = pl.DeviceIdType.MESH
 F32 = jnp.float32
 BF16 = jnp.bfloat16
@@ -67,10 +68,14 @@
     ro_x=pltpu.VMEM((3, 4, 16, ZD // 2), BF16),
     gl_z=pltpu.VMEM((4, 32, PH // 2), BF16),
     go_z=pltpu.VMEM((4, 16, ZD // 2), BF16),
-    rl_z=pltpu.VMEM((7, 32, PH // 2), BF16),
-    ro_z=pltpu.VMEM((7, 16, ZD // 2), BF16),
-    pl_f=pltpu.VMEM((32, PH // 2), F32),
-    po_f=pltpu.VMEM((16, ZD // 2), F32),
+    rl_z=pltpu.VMEM((3, 32, PH // 2), BF16),
+    ro_z=pltpu.VMEM((3, 16, ZD // 2), BF16),
+    hl_z=pltpu.VMEM((2, 32, PH // 2), BF16),
+    ho_z=pltpu.VMEM((2, 16, ZD // 2), BF16),
+    pl_f=pltpu.VMEM((32, PH // 2), BF16),
+    po_f=pltpu.VMEM((16, ZD // 2), BF16),
+    lift_sum=pltpu.VMEM((128, PH), BF16),
+    out_sum=pltpu.VMEM((64, ZD), BF16),
     s_a2a=pltpu.SemaphoreType.DMA((8, 16)),
     r_a2a=pltpu.SemaphoreType.DMA((8, 16)),
     s_rel=pltpu.SemaphoreType.DMA((16,)),
@@ -324,32 +329,44 @@
 
     for wait in along_z:
         wait()
-    along_y = []
-    for n, (_, full, height, width) in enumerate(weights):
-        rows = pl.ds(pl.multiple_of(c * height, height), height)
-        part = pl.ds(pl.multiple_of(y * width, 128), width)
-        for i in range(1, 4):
-            piece = full.at[:, x, rows, part]
-            along_y.append(
-                go(piece, piece, s["s_w"].at[n, 2 + i], s["r_w"].at[n, 2 + i], at_y(i))
-            )
-    for copy in along_y:
-        copy.wait_recv()
-    along_x, to_core = [], []
-
-    def core_piece(n, i):
-        _, full, height, _ = weights[n]
-        piece = full.at[:, lax.rem(x + 4 - i, 4), pl.ds(pl.multiple_of(c * height, height), height), :]
-        to_core.append(go(piece, piece, s["s_w"].at[n, 9 + i], s["r_w"].at[n, 9 + i], partner))
-
-    for n, (_, full, height, _) in enumerate(weights):
-        rows = pl.ds(pl.multiple_of(c * height, height), height)
-        for i in range(1, 4):
-            piece = full.at[:, x, rows, :]
-            along_x.append(
-                (n, i, go(piece, piece, s["s_w"].at[n, 5 + i], s["r_w"].at[n, 5 + i], at_x(i)))
-            )
-        core_piece(n, 0)
+    def second(n, i, piece, device):
+        return go(piece, piece, s["s_w"].at[n, i], s["r_w"].at[n, i], device)
+
+    lift_rows = pl.ds(pl.multiple_of(c * 64, 64), 64)
+    out_rows = pl.ds(pl.multiple_of(c * 32, 32), 32)
+
+    def lift_cols(at):
+        return pl.ds(pl.multiple_of(lax.rem(at, 4) * 256, 128), 256)
+
+    def out_cols(at):
+        return pl.ds(pl.multiple_of(lax.rem(at, 4) * 384, 128), 384)
+
+    lift_y = [
+        second(0, 2 + i, s["liftf"].at[:, x, lift_rows, lift_cols(y)], at_y(i))
+        for i in range(1, 4)
+    ]
+    out_x = [
+        second(1, 2 + i, s["outf"].at[:, x, out_rows, out_cols(y)], at_x(i))
+        for i in range(1, 4)
+    ]
+
+    def lift_to_core(i):
+        return second(0, 9 + i, s["liftf"].at[:, lax.rem(x + 4 - i, 4), lift_rows, :], partner)
+
+    def out_to_core(i):
+        return second(1, 9 + i, s["outf"].at[:, :, out_rows, out_cols(y + 4 - i)], partner)
+
+    for copy in lift_y:
+        copy.wait_recv()
+    lift_x = [
+        second(0, 5 + i, s["liftf"].at[:, x, lift_rows, :], at_x(i)) for i in range(1, 4)
+    ]
+    for copy in out_x:
+        copy.wait_recv()
+    out_y = [
+        second(1, 5 + i, s["outf"].at[:, :, out_rows, out_cols(y)], at_y(i)) for i in range(1, 4)
+    ]
+    lift_core, out_core = [lift_to_core(0)], [out_to_core(0)]
 
     got_gate()
     gating = dot(s["emb"][...].astype(BF16), s["gcols"][...], ((1,), (0,)))[0:1]
@@ -382,9 +399,12 @@
         return 0
 
     lax.fori_loop(0, LEN // QB, forward, 0)
-    for n, i, copy in along_x:
-        copy.wait_recv()
-        core_piece(n, i)
+    for i, copy in enumerate(lift_x):
+        copy.wait_recv()
+        lift_core.append(lift_to_core(i + 1))
+    for i, copy in enumerate(out_y):
+        copy.wait_recv()
+        out_core.append(out_to_core(i + 1))
 
     def relay_wait(i, _):
         j = lax.rem(me + i, 16)
@@ -405,7 +425,7 @@
         go(s["hid2"].at[0:TOK, :], s["hid2"].at[TOK:, :],
            s["s_pair"].at[0], s["r_pair"].at[0], partner)
     ]
-    for copy in to_core:
+    for copy in lift_core:
         copy.wait_recv()
     lifted = jnp.zeros((TOK, PH), F32)
     for i in range(4):
@@ -420,6 +440,8 @@
         go(s["act2"].at[0:TOK, :], s["act2"].at[TOK:, :],
            s["s_pair"].at[1], s["r_pair"].at[1], partner)
     )
+    for copy in out_core:
+        copy.wait_recv()
     predicted = jnp.zeros((TOK, ZD), F32)
     for i in range(4):
         predicted += dot(
@@ -530,7 +552,7 @@
         s["dq32"][...] += dot(grad_scores, keys, ((0,), (0,)))
         return 0
 
-    lax.fori_loop(0, LEN // KB // 2, backward, 0)
+    lax.fori_loop(0, EARLY, backward, 0)
 
     for copy in sums:
         copy.wait_recv()
@@ -548,7 +570,7 @@
             go(s["go_y"].at[:, lax.rem(x + i, 4)], s["ro_x"].at[i - 1],
                s["s_red"].at[1, 2 + i], s["r_red"].at[1, 2 + i], at_x(i))
         )
-    lax.fori_loop(LEN // KB // 2, LEN // KB, backward, 0)
+    lax.fori_loop(EARLY, LEN // KB, backward, 0)
     s["dqb"][...] = (s["dq32"][...] * SCALE).astype(BF16)
 
     def send_queries(i, _):
@@ -564,10 +586,10 @@
     s["go_z"][...] = total(s["go_y"][:, x], s["ro_x"]).astype(BF16)
     sums = []
     for n, (part, room) in enumerate([("gl_z", "rl_z"), ("go_z", "ro_z")]):
-        for i in range(1, 8):
+        for i, hop in enumerate((1, 7, 2 + 4 * c)):
             sums.append(
-                go(s[part].at[lax.rem(z + i, 4)], s[room].at[i - 1],
-                   s["s_red"].at[n, 5 + i], s["r_red"].at[n, 5 + i], at_z(i))
+                go(s[part].at[lax.rem(z + hop, 4)], s[room].at[i],
+                   s["s_red"].at[n, 6 + i], s["r_red"].at[n, 6 + i], at_z(hop))
             )
 
     got_emb()
@@ -584,26 +606,37 @@
     for copy in sums:
         copy.wait_recv()
     sums = []
+    halves = [("gl_z", "rl_z", "hl_z"), ("go_z", "ro_z", "ho_z")]
+    for n, (part, room, side) in enumerate(halves):
+        s[side][0] = total(s[part][zl], s[room]).astype(BF16)
+        sums.append(
+            go(s[side].at[0], s[side].at[1], s["s_red"].at[n, 9], s["r_red"].at[n, 9], at_z(4))
+        )
+    for copy in sums:
+        copy.wait_recv()
+    sums = []
     final = [
-        ("gl_z", "rl_z", "pl_f", glift, 32, PH // 2),
-        ("go_z", "ro_z", "po_f", gout, 16, ZD // 2),
+        ("hl_z", "pl_f", "lift_sum", 32, PH // 2),
+        ("ho_z", "po_f", "out_sum", 16, ZD // 2),
     ]
-    for n, (part, room, piece, whole, height, width) in enumerate(final):
-        s[piece][...] = total(s[part][zl], s[room])
-        to = whole.at[
-            pl.ds(pl.multiple_of(y * height, height), height),
-            pl.ds(pl.multiple_of(c * width, 128), width),
-        ]
-        own = pltpu.make_async_copy(s[piece], to, s["local"].at[15 + n])
-        own.start()
-        finish.append(own.wait)
+    for n, (side, piece, whole, height, width) in enumerate(final):
+        added = (s[side][0].astype(F32) + s[side][1].astype(F32)).astype(BF16)
+        s[piece][...] = added
+        rows = pl.ds(pl.multiple_of(y * height, height), height)
+        part = pl.ds(pl.multiple_of(c * width, 128), width)
+        s[whole][rows, part] = added
         for i in range(1, 8):
             sums.append(
-                go(s[piece], to, s["s_red"].at[n, 12 + i], s["r_red"].at[n, 12 + i], at_yc(i))
+                go(s[piece], s[whole].at[rows, part],
+                   s["s_red"].at[n, 12 + i], s["r_red"].at[n, 12 + i], at_yc(i))
             )
     got_ggate()
     for copy in sums:
         copy.wait_recv()
+    for whole, out, n in (("lift_sum", glift, 15), ("out_sum", gout, 16)):
+        own = pltpu.make_async_copy(s[whole], out, s["local"].at[n])
+        own.start()
+        finish.append(own.wait)
     got_dk()
     got_dv()
     got_dq()
@@ -612,14 +645,8 @@
 
 
 def copy_kernel(*refs):
-    sems = refs[-1]
-    copies = [
-        pltpu.make_async_copy(refs[i], refs[6 + i], sems.at[i]) for i in range(6)
-    ]
-    for copy in copies:
-        copy.start()
-    for copy in copies:
-        copy.wait()
+    for i in range(6):
+        refs[6 + i][...] = refs[i][...].astype(refs[6 + i].dtype)
 
 
 def shards(
@@ -647,7 +674,8 @@
     )
     outs = pl.pallas_call(
         step_kernel,
-        out_shape=out_shape,
+        out_shape=out_shape[:4]
+        + (jax.ShapeDtypeStruct((128, PH), BF16), jax.ShapeDtypeStruct((64, ZD), BF16)),
         in_specs=[anywhere] * 3 + [near] * 5 + [pl.BlockSpec(memory_space=pltpu.SMEM)]
         + [anywhere] * 3,
         out_specs=(anywhere,) * 6,
@@ -663,9 +691,10 @@
     d_queries, d_keys, d_values, grad_gate, grad_lift, grad_out = pl.pallas_call(
         copy_kernel,
         out_shape=out_shape,
-        in_specs=[anywhere] * 6,
-        out_specs=(anywhere,) * 6,
-        scratch_shapes=[pltpu.SemaphoreType.DMA((6,))],
+        grid=(2,),
+        in_specs=[pl.BlockSpec((a.shape[0] // 2, a.shape[1]), lambda i: (i, 0)) for a in out_shape],
+        out_specs=[pl.BlockSpec((a.shape[0] // 2, a.shape[1]), lambda i: (i, 0)) for a in out_shape],
+        compiler_params=pltpu.CompilerParams(vmem_limit_bytes=32 << 20),
         name="hand_out",
     )(*outs)
     return (d_queries[None], d_keys[None], d_values[None], grad_gate, grad_lift, grad_out)

time: 274 us -> 187 us (0.68); the launches traced: 270 us -> 187 us
  Pallas kernels: 268 us -> 180 us
  local copies, waits for them, and re-layouts: 0 us -> 5.9 us
    pallas_call x2, Pallas kernels: 268 us -> 180 us  [the longest x1 178 us: shards(): pl.pallas_call(step_kernel, out_shape=out_shape[:4] + (jax.ShapeDtypeStru...]
    unnamed x0 -> x12, local copies, waits for them, and re-layouts: none -> 5.9 us
where the time goes in v3:
time: 187 us
  Pallas kernels  180 us (96%)
  local copies, waits for them, and re-layouts  5.9 us (3%)
    pallas_call x1, Pallas kernels, shards(): pl.pallas_call(step_kernel, out_shape=out_shape[:4] + (jax.ShapeDtypeStru...  178 us
    unnamed x12, local copies, waits for them, and re-layouts  5.9 us

profile of v3, /device:TPU:1, one launch (start us, length us, event | category | flops | bytes accessed | tf_op | source)
XLA Modules:
  0.0 186.9 jit_solution(6388657446611362669)
XLA Ops:
  1.3 178.2 %repa_step.1 = (bf16[128,2048]{1,0:T(8,128)(2,1)}, bf16[128,2048]{1,0:T(8,128)(2,1)}, bf16[128,2048]{1,0:T(8,128)(2,1)}, f32[16,2048]{1,0:T(8,128)}, bf16[128,10...) custom-call(bf16[128,2048]{1,0:T(8,128)(2,1)} %bitcast.8, bf16[128,2048]{1,0:T(8,128)(2,1)} %bitcast.9, ...), custom_call_target="tpu_custom_call" | custom-call | tf_op jit(solution)/shard_map/repa_step/pallas_call | solution.py:675
  179.5 0.0 copy-start
  179.5 1.0 copy-done
  180.5 0.0 copy-start.1
  180.5 1.0 copy-done.1
  181.6 0.0 copy-start.2
  181.6 1.0 copy-done.2
  182.6 0.0 copy-start.3
  182.6 0.9 copy-done.3
  183.6 0.0 copy-start.4
  183.6 0.9 copy-done.4
  184.5 0.0 copy-start.5
  184.5 0.9 copy-done.5
  185.4 1.5 hand_out.1
Async XLA Ops:
  179.5 1.0 copy-start
  180.5 1.0 copy-start.1
  181.6 1.0 copy-start.2
  182.6 0.9 copy-start.3
  183.6 0.9 copy-start.4
  184.5 0.9 copy-start.5

commit v4 on v3

--- a/solution.py
+++ b/solution.py
@@ -166,13 +166,22 @@
                 s["s_a2a"].at[t, j], s["r_a2a"].at[t, owner], (dp, j),
             )
 
-        def start(i, _):
-            copy(lax.rem(me + i, 16), me).start()
+        def far(i, _):
+            copy((1 - zh) * 8 + lax.rem(yc + i, 8), me).start()
             return 0
 
+        def near(i, _):
+            copy(zh * 8 + lax.rem(yc + i, 8), me).start()
+            return 0
+
         own = pltpu.make_async_copy(src.at[:, cols(me)], dst.at[cols(me), :], s["local"].at[t])
-        own.start()
-        lax.fori_loop(1, 16, start, 0)
+
+        def start_far():
+            lax.fori_loop(0, 8, far, 0)
+
+        def start_near():
+            own.start()
+            lax.fori_loop(1, 8, near, 0)
 
         def wait():
             def one(i, _):
@@ -191,7 +200,7 @@
             lax.fori_loop(1, 16, one, 0)
 
         finish.append(sent)
-        return wait
+        return start_far, start_near, wait
 
     def head_to_tok(t, src, dst):
         def copy(j, owner):
@@ -280,9 +289,11 @@
         )
         own.start()
         along_z.append(own.wait)
-    got_q = tok_to_head(0, q, s["qh"])
-    got_k = tok_to_head(1, k, s["kh"])
-    got_v = tok_to_head(2, v, s["vh"])
+    far_q, near_q, got_q = tok_to_head(0, q, s["qh"])
+    far_k, near_k, got_k = tok_to_head(1, k, s["kh"])
+    far_v, near_v, got_v = tok_to_head(2, v, s["vh"])
+    for start in (far_q, far_k, far_v, near_q, near_k, near_v):
+        start()
     got_gate = spread(
         0, lambda j: gate.at[:, cols(me)],
         lambda j: s["gcols"].at[pl.ds(pl.multiple_of(j * 16, 16), 16), :], dp,
@@ -314,8 +325,12 @@
             s["s_rel"].at[j], s["r_rel"].at[owner], (dp, j),
         )
 
-    def relay_start(i, _):
-        relay(lax.rem(me + i, 16), me).start()
+    def relay_near(i, _):
+        relay(zh * 8 + lax.rem(yc + i, 8), me).start()
+        return 0
+
+    def relay_far(i, _):
+        relay((1 - zh) * 8 + lax.rem(yc + i, 8), me).start()
         return 0
 
     def relay_sent():
@@ -373,7 +388,7 @@
     got_q()
     got_k()
     got_v()
-    lax.fori_loop(1, 16, relay_start, 0)
+    lax.fori_loop(1, 8, relay_near, 0)
     mine = pl.ds(pl.multiple_of(me * 16, 16), 16)
     relay_own = pltpu.make_async_copy(
         s["rows_send"].at[mine, :], s["rows_got"].at[mine, :], s["local"].at[14]
@@ -399,24 +414,13 @@
         return 0
 
     lax.fori_loop(0, LEN // QB, forward, 0)
+    lax.fori_loop(0, 8, relay_far, 0)
     for i, copy in enumerate(lift_x):
         copy.wait_recv()
         lift_core.append(lift_to_core(i + 1))
     for i, copy in enumerate(out_y):
         copy.wait_recv()
         out_core.append(out_to_core(i + 1))
-
-    def relay_wait(i, _):
-        j = lax.rem(me + i, 16)
-        relay(j, j).wait_recv()
-        return 0
-
-    relay_own.wait()
-    lax.fori_loop(1, 16, relay_wait, 0)
-    tokens = lax.broadcasted_iota(jnp.int32, (256, TOK), 1).astype(F32) + 1.0
-    placed = jnp.where(s["rows_got"][:, ZD : ZD + 1].astype(F32) == tokens, 1.0, 0.0).astype(BF16)
-    target = dot(placed, s["rows_got"][:, :ZD], ((0,), (0,)))
-    target_norm = jnp.sqrt(jnp.sum(target * target, axis=1, keepdims=True) + EPSILON)
 
     got_mix()
     hidden = (res[...].astype(F32) + s["mix_tok"][...].astype(F32)).astype(BF16)
@@ -448,6 +452,18 @@
             s["act2"][0:TOK, i * 256 : (i + 1) * 256],
             s["outf"][i].reshape(256, ZD), ((1,), (0,)),
         )
+    def relay_wait(i, _):
+        j = lax.rem(me + i, 16)
+        relay(j, j).wait_recv()
+        return 0
+
+    relay_own.wait()
+    lax.fori_loop(1, 16, relay_wait, 0)
+    tokens = lax.broadcasted_iota(jnp.int32, (256, TOK), 1).astype(F32) + 1.0
+    placed = jnp.where(s["rows_got"][:, ZD : ZD + 1].astype(F32) == tokens, 1.0, 0.0).astype(BF16)
+    target = dot(placed, s["rows_got"][:, :ZD], ((0,), (0,)))
+    target_norm = jnp.sqrt(jnp.sum(target * target, axis=1, keepdims=True) + EPSILON)
+
     pred_norm = jnp.sqrt(jnp.sum(predicted * predicted, axis=1, keepdims=True) + EPSILON)
     both = pred_norm * target_norm
     cosine = jnp.sum(predicted * target, axis=1, keepdims=True) / both
@@ -473,7 +489,9 @@
         s["ghs"][:, i * 512 : (i + 1) * 512] = dot(
             grad_lifted, s["liftf"][i].reshape(512, PH), ((1,), (1,))
         ).astype(BF16)
-    got_grad = tok_to_head(4, s["ghs"], s["gh"])
+    far_grad, near_grad, got_grad = tok_to_head(4, s["ghs"], s["gh"])
+    far_grad()
+    near_grad()
 
     s["gp2"][0:TOK, :] = s["gpf"][c]
     s["gl2"][0:TOK, :] = s["glf"][c]
@@ -515,7 +533,7 @@
         return added
 
     got_grad()
-    ones = jnp.ones((8, HD), F32)
+    ones = jnp.ones((8, HD), BF16)
 
     def prepare(i, partial):
         at = pl.ds(pl.multiple_of(i * QB, QB), QB)
@@ -523,9 +541,10 @@
         mixed = s["o32"][at, :]
         scaled = (gating * grad).astype(BF16)
         s["do"][at, :] = scaled
-        s["drow"][:, at] = dot(
-            ones, scaled.astype(F32) * mixed, ((1,), (1,)), lax.Precision.HIGHEST
-        )
+        inner = scaled.astype(F32) * mixed
+        upper = inner.astype(BF16)
+        lower = (inner - upper.astype(F32)).astype(BF16)
+        s["drow"][:, at] = dot(ones, upper, ((1,), (1,))) + dot(ones, lower, ((1,), (1,)))
         product = grad * mixed.astype(BF16).astype(F32)
         return partial + jnp.sum(product.reshape(QB // 8, 8, HD), axis=0)
 
@@ -571,14 +590,6 @@
                s["s_red"].at[1, 2 + i], s["r_red"].at[1, 2 + i], at_x(i))
         )
     lax.fori_loop(EARLY, LEN // KB, backward, 0)
-    s["dqb"][...] = (s["dq32"][...] * SCALE).astype(BF16)
-
-    def send_queries(i, _):
-        send_dq(lax.rem(me + i, 16))
-        return 0
-
-    lax.fori_loop(0, 16, send_queries, 0)
-
     for copy in sums:
         copy.wait_recv()
     y_rows = pl.ds(pl.multiple_of(y * 32, 32), 32)
@@ -591,6 +602,15 @@
                 go(s[part].at[lax.rem(z + hop, 4)], s[room].at[i],
                    s["s_red"].at[n, 6 + i], s["r_red"].at[n, 6 + i], at_z(hop))
             )
+
+    s["dqb"][...] = (s["dq32"][...] * SCALE).astype(BF16)
+
+    def send_queries(i, _):
+        half = lax.rem(1 - zh + lax.div(i, 8), 2)
+        send_dq(half * 8 + lax.rem(yc + i, 8))
+        return 0
+
+    lax.fori_loop(0, 16, send_queries, 0)
 
     got_emb()
     got_gg()
@@ -694,7 +714,7 @@
         grid=(2,),
         in_specs=[pl.BlockSpec((a.shape[0] // 2, a.shape[1]), lambda i: (i, 0)) for a in out_shape],
         out_specs=[pl.BlockSpec((a.shape[0] // 2, a.shape[1]), lambda i: (i, 0)) for a in out_shape],
-        compiler_params=pltpu.CompilerParams(vmem_limit_bytes=32 << 20),
+        compiler_params=pltpu.CompilerParams(vmem_limit_bytes=60 << 20),
         name="hand_out",
     )(*outs)
     return (d_queries[None], d_keys[None], d_values[None], grad_gate, grad_lift, grad_out)

time: 187 us -> 186 us (level); the launches traced: 187 us -> 183 us
  local copies, waits for them, and re-layouts: 5.9 us -> 0 us
  Pallas kernels: 180 us -> 182 us
    unnamed x12 -> x0, local copies, waits for them, and re-layouts: 5.9 us -> none
where the time goes in v4:
time: 186 us; the launch traced here: 183 us
  Pallas kernels  182 us (98%)
    pallas_call x1, Pallas kernels, shards(): pl.pallas_call(step_kernel, out_shape=out_shape[:4] + (jax.ShapeDtypeStru...  179 us

profile of v4, /device:TPU:1, one launch (start us, length us, event | category | flops | bytes accessed | tf_op | source)
XLA Modules:
  0.0 183.2 jit_solution(1007082033026768873)
XLA Ops:
  1.3 179.2 %repa_step.1 = (bf16[128,2048]{1,0:T(8,128)(2,1)}, bf16[128,2048]{1,0:T(8,128)(2,1)}, bf16[128,2048]{1,0:T(8,128)(2,1)}, f32[16,2048]{1,0:T(8,128)}, bf16[128,10...) custom-call(bf16[128,2048]{1,0:T(8,128)(2,1)} %bitcast.8, bf16[128,2048]{1,0:T(8,128)(2,1)} %bitcast.9, ...), custom_call_target="tpu_custom_call" | custom-call | tf_op jit(solution)/shard_map/repa_step/pallas_call | solution.py:695
  180.5 2.8 %hand_out.1 = (bf16[128,2048]{1,0:T(8,128)(2,1)}, bf16[128,2048]{1,0:T(8,128)(2,1)}, bf16[128,2048]{1,0:T(8,128)(2,1)}, f32[16,2048]{1,0:T(8,128)}, f32[128,1024]{1,0:T(8,128)}, /*index=5*/f32[64,1536]{1,0:T(8,128)}) custom-call(bf16[128,2048]{1,0:T(8,128)(2,1)} %get-tuple-element.18.refs_0_, bf16[128,2048]{1,0:T(8,128)(2,1)} %get-tuple-element.19.refs_1_, ...), custom_call_target="tpu_custom_call" | custom-call | tf_op jit(solution)/shard_map/hand_out/pallas_call | solution.py:711

commit v5 on v4

--- a/solution.py
+++ b/solution.py
@@ -46,6 +46,7 @@
     gp2=pltpu.VMEM((2 * TOK, ZD // 2), BF16),
     glf=pltpu.VMEM((2, TOK, PH // 2), BF16),
     gl2=pltpu.VMEM((2 * TOK, PH // 2), BF16),
+    glw=pltpu.VMEM((TOK, PH), BF16),
     ghs=pltpu.VMEM((TOK, FEAT), BF16),
     gh=pltpu.VMEM((LEN, HD), BF16),
     do=pltpu.VMEM((LEN, HD), BF16),
@@ -167,14 +168,23 @@
             )
 
         def far(i, _):
-            copy((1 - zh) * 8 + lax.rem(yc + i, 8), me).start()
+            copy(lax.rem(me + i + 8, 16), me).start()
             return 0
 
         def near(i, _):
-            copy(zh * 8 + lax.rem(yc + i, 8), me).start()
+            copy(lax.rem(me + i, 16), me).start()
             return 0
 
         own = pltpu.make_async_copy(src.at[:, cols(me)], dst.at[cols(me), :], s["local"].at[t])
+
+        def send(j):
+            @pl.when(j != me)
+            def _():
+                copy(j, me).start()
+
+            @pl.when(j == me)
+            def _():
+                own.start()
 
         def start_far():
             lax.fori_loop(0, 8, far, 0)
@@ -200,7 +210,7 @@
             lax.fori_loop(1, 16, one, 0)
 
         finish.append(sent)
-        return start_far, start_near, wait
+        return start_far, start_near, send, wait
 
     def head_to_tok(t, src, dst):
         def copy(j, owner):
@@ -289,10 +299,10 @@
         )
         own.start()
         along_z.append(own.wait)
-    far_q, near_q, got_q = tok_to_head(0, q, s["qh"])
-    far_k, near_k, got_k = tok_to_head(1, k, s["kh"])
-    far_v, near_v, got_v = tok_to_head(2, v, s["vh"])
-    for start in (far_q, far_k, far_v, near_q, near_k, near_v):
+    far_q, near_q, _, got_q = tok_to_head(0, q, s["qh"])
+    far_k, near_k, _, got_k = tok_to_head(1, k, s["kh"])
+    far_v, near_v, _, got_v = tok_to_head(2, v, s["vh"])
+    for start in (near_q, far_q, near_k, far_k, near_v, far_v):
         start()
     got_gate = spread(
         0, lambda j: gate.at[:, cols(me)],
@@ -342,6 +352,14 @@
 
     finish.append(relay_sent)
 
+    lax.fori_loop(1, 8, relay_near, 0)
+    lax.fori_loop(0, 8, relay_far, 0)
+    mine = pl.ds(pl.multiple_of(me * 16, 16), 16)
+    relay_own = pltpu.make_async_copy(
+        s["rows_send"].at[mine, :], s["rows_got"].at[mine, :], s["local"].at[14]
+    )
+    relay_own.start()
+
     for wait in along_z:
         wait()
     def second(n, i, piece, device):
@@ -388,13 +406,6 @@
     got_q()
     got_k()
     got_v()
-    lax.fori_loop(1, 8, relay_near, 0)
-    mine = pl.ds(pl.multiple_of(me * 16, 16), 16)
-    relay_own = pltpu.make_async_copy(
-        s["rows_send"].at[mine, :], s["rows_got"].at[mine, :], s["local"].at[14]
-    )
-    relay_own.start()
-
     send_mix, got_mix = head_to_tok(3, s["gated"], s["mix_tok"])
 
     def forward(i, _):
@@ -414,7 +425,6 @@
         return 0
 
     lax.fori_loop(0, LEN // QB, forward, 0)
-    lax.fori_loop(0, 8, relay_far, 0)
     for i, copy in enumerate(lift_x):
         copy.wait_recv()
         lift_core.append(lift_to_core(i + 1))
@@ -485,13 +495,19 @@
         go(s["glf"].at[1 - c], s["gl2"].at[TOK:, :], s["s_pair"].at[3], s["r_pair"].at[3], partner)
     )
     grad_lifted = jnp.concatenate([s["glf"][0], s["glf"][1]], axis=1)
-    for i in range(4):
-        s["ghs"][:, i * 512 : (i + 1) * 512] = dot(
-            grad_lifted, s["liftf"][i].reshape(512, PH), ((1,), (1,))
+    s["glw"][...] = grad_lifted
+    _, _, send_grad, got_grad = tok_to_head(4, s["ghs"], s["gh"])
+
+    def hidden_part(i, _):
+        group = lax.rem(lax.div(me, 4) + i, 4)
+        s["ghs"][:, pl.ds(pl.multiple_of(group * 512, 512), 512)] = dot(
+            s["glw"][...], s["liftf"][group].reshape(512, PH), ((1,), (1,))
         ).astype(BF16)
-    far_grad, near_grad, got_grad = tok_to_head(4, s["ghs"], s["gh"])
-    far_grad()
-    near_grad()
+        for r in range(4):
+            send_grad(group * 4 + lax.rem(me + r, 4))
+        return 0
+
+    lax.fori_loop(0, 4, hidden_part, 0)
 
     s["gp2"][0:TOK, :] = s["gpf"][c]
     s["gl2"][0:TOK, :] = s["glf"][c]
@@ -573,6 +589,17 @@
 
     lax.fori_loop(0, EARLY, backward, 0)
 
+    got_emb()
+    got_gg()
+    s["gfull"][...] = dot(
+        s["embs"][...].reshape(128, TEMB), s["ggall"][...].reshape(128, HD), ((0,), (0,)),
+        lax.Precision.HIGHEST,
+    )
+    s["gsl"][...] = s["gfull"][pl.ds(pl.multiple_of(dp * 16, 16), 16), :]
+    got_ggate = spread(
+        3, lambda j: s["gsl"], lambda j: ggate.at[:, cols(j)], me, lambda j: (dp, j)
+    )
+
     for copy in sums:
         copy.wait_recv()
     s["gl_y"][...] = total(s["gl_x"][:, x], s["rl_x"]).astype(BF16)
@@ -611,17 +638,6 @@
         return 0
 
     lax.fori_loop(0, 16, send_queries, 0)
-
-    got_emb()
-    got_gg()
-    s["gfull"][...] = dot(
-        s["embs"][...].reshape(128, TEMB), s["ggall"][...].reshape(128, HD), ((0,), (0,)),
-        lax.Precision.HIGHEST,
-    )
-    s["gsl"][...] = s["gfull"][pl.ds(pl.multiple_of(dp * 16, 16), 16), :]
-    got_ggate = spread(
-        3, lambda j: s["gsl"], lambda j: ggate.at[:, cols(j)], me, lambda j: (dp, j)
-    )
 
     for copy in sums:
         copy.wait_recv()

time: 186 us -> 179 us (0.962)
  Pallas kernels: 182 us -> 174 us
    pallas_call x1, Pallas kernels: 179 us -> 171 us  [shards(): pl.pallas_call(step_kernel, out_shape=out_shape[:4] + (jax.ShapeDtypeStru...]
where the time goes in v5:
time: 179 us; the launch traced here: 175 us
  Pallas kernels  174 us (97%)
    pallas_call x1, Pallas kernels, shards(): pl.pallas_call(step_kernel, out_shape=out_shape[:4] + (jax.ShapeDtypeStru...  171 us

profile of v5, /device:TPU:1, one launch (start us, length us, event | category | flops | bytes accessed | tf_op | source)
XLA Modules:
  0.0 175.4 jit_solution(10574684477694816878)
XLA Ops:
  1.3 171.4 %repa_step.1 = (bf16[128,2048]{1,0:T(8,128)(2,1)}, bf16[128,2048]{1,0:T(8,128)(2,1)}, bf16[128,2048]{1,0:T(8,128)(2,1)}, f32[16,2048]{1,0:T(8,128)}, bf16[128,10...) custom-call(bf16[128,2048]{1,0:T(8,128)(2,1)} %bitcast.8, bf16[128,2048]{1,0:T(8,128)(2,1)} %bitcast.9, ...), custom_call_target="tpu_custom_call" | custom-call | tf_op jit(solution)/shard_map/repa_step/pallas_call | solution.py:711
  172.7 2.8 %hand_out.1 = (bf16[128,2048]{1,0:T(8,128)(2,1)}, bf16[128,2048]{1,0:T(8,128)(2,1)}, bf16[128,2048]{1,0:T(8,128)(2,1)}, f32[16,2048]{1,0:T(8,128)}, f32[128,1024]{1,0:T(8,128)}, /*index=5*/f32[64,1536]{1,0:T(8,128)}) custom-call(bf16[128,2048]{1,0:T(8,128)(2,1)} %get-tuple-element.18.refs_0_, bf16[128,2048]{1,0:T(8,128)(2,1)} %get-tuple-element.19.refs_1_, ...), custom_call_target="tpu_custom_call" | custom-call | tf_op jit(solution)/shard_map/hand_out/pallas_call | solution.py:727

commit v6 on v5

--- a/solution.py
+++ b/solution.py
@@ -20,7 +20,7 @@
 LOG2 = SCALE * math.log2(math.e)
 QB = 256
 KB = 256
-EARLY = 6
+EARLY = 7
 MESH = pl.DeviceIdType.MESH
 F32 = jnp.float32
 BF16 = jnp.bfloat16
@@ -617,6 +617,15 @@
                s["s_red"].at[1, 2 + i], s["r_red"].at[1, 2 + i], at_x(i))
         )
     lax.fori_loop(EARLY, LEN // KB, backward, 0)
+    s["dqb"][...] = (s["dq32"][...] * SCALE).astype(BF16)
+
+    def send_queries(i, _):
+        half = lax.rem(1 - zh + lax.div(i, 8), 2)
+        send_dq(half * 8 + lax.rem(yc + i, 8))
+        return 0
+
+    lax.fori_loop(0, 16, send_queries, 0)
+
     for copy in sums:
         copy.wait_recv()
     y_rows = pl.ds(pl.multiple_of(y * 32, 32), 32)
@@ -629,15 +638,6 @@
                 go(s[part].at[lax.rem(z + hop, 4)], s[room].at[i],
                    s["s_red"].at[n, 6 + i], s["r_red"].at[n, 6 + i], at_z(hop))
             )
-
-    s["dqb"][...] = (s["dq32"][...] * SCALE).astype(BF16)
-
-    def send_queries(i, _):
-        half = lax.rem(1 - zh + lax.div(i, 8), 2)
-        send_dq(half * 8 + lax.rem(yc + i, 8))
-        return 0
-
-    lax.fori_loop(0, 16, send_queries, 0)
 
     for copy in sums:
         copy.wait_recv()

time: 179 us -> 177 us (0.989); the launches traced: 175 us -> 177 us
  no operation moved by 1% of the time
where the time goes in v6:
time: 177 us
  Pallas kernels  175 us (99%)
    pallas_call x1, Pallas kernels, shards(): pl.pallas_call(step_kernel, out_shape=out_shape[:4] + (jax.ShapeDtypeStru...  173 us

profile of v6, /device:TPU:1, one launch (start us, length us, event | category | flops | bytes accessed | tf_op | source)
XLA Modules:
  0.0 176.7 jit_solution(3537782372996202144)
XLA Ops:
  1.3 172.6 %repa_step.1 = (bf16[128,2048]{1,0:T(8,128)(2,1)}, bf16[128,2048]{1,0:T(8,128)(2,1)}, bf16[128,2048]{1,0:T(8,128)(2,1)}, f32[16,2048]{1,0:T(8,128)}, bf16[128,10...) custom-call(bf16[128,2048]{1,0:T(8,128)(2,1)} %bitcast.8, bf16[128,2048]{1,0:T(8,128)(2,1)} %bitcast.9, ...), custom_call_target="tpu_custom_call" | custom-call | tf_op jit(solution)/shard_map/repa_step/pallas_call | solution.py:711
  173.9 2.8 %hand_out.1 = (bf16[128,2048]{1,0:T(8,128)(2,1)}, bf16[128,2048]{1,0:T(8,128)(2,1)}, bf16[128,2048]{1,0:T(8,128)(2,1)}, f32[16,2048]{1,0:T(8,128)}, f32[128,1024]{1,0:T(8,128)}, /*index=5*/f32[64,1536]{1,0:T(8,128)}) custom-call(bf16[128,2048]{1,0:T(8,128)(2,1)} %get-tuple-element.18.refs_0_, bf16[128,2048]{1,0:T(8,128)(2,1)} %get-tuple-element.19.refs_1_, ...), custom_call_target="tpu_custom_call" | custom-call | tf_op jit(solution)/shard_map/hand_out/pallas_call | solution.py:727
